TPU v7x, 32 devices: a whole 2x2x4 slice. The times are simulated.
32 devices in a mesh: group: 2 (over y), patch: 4 (over z), section: 4 (over x, core).
Axes of the slice: x: 2, y: 2, z: 4, core: 2. Of those that a mesh axis runs over, the one named last changes fastest.
Arguments:
- hidden: bfloat16 [4, 8, 2560], P('section', 'patch'), may hold values from -6 to 6
- kv_cache: bfloat16 [4, 64, 2, 2560], P('section', ('group', 'patch')), parts along dimension 1, may hold values from -7 to 7
- step_index: int32 [8], P('group'), parts along dimension 0, may hold values from 0 to 14
- mod_table: float32 [16, 4, 3, 2560], P(None, 'section'), may hold values from -4 to 4
- query_gain: float32 [4, 2560], P('section'), may hold values from -6 to 6
- key_gain: float32 [4, 2560], P('section'), may hold values from -6 to 6
Outputs:
- hidden_out: bfloat16 [4, 16, 2560], P('section', ('group', 'patch')), parts along dimension 1
- cache_out: bfloat16 [4, 64, 2, 2560], P('section', ('group', 'patch')), parts along dimension 1
There are 2 independent parts, one for each index of `group`. A program takes and returns all parts, laid end to end along the dimension named above; an argument that names none is the same for every part. Nothing has to cross between parts.
All inputs are finite; a program needn't handle non-finite values.
Results may differ from a plain program's by a relative error of at most 0.025.
Values may be sent and summed in bfloat16 or wider, within the bound.
No kernel may reach another device: no remote copies, remote signals or barrier semaphores. Data moves between devices by JAX's collectives and lax.ppermute only.
A program may use at most 64 MiB of HBM per device.

v0:
```python
import jax
import jax.numpy as jnp
from jax import lax
from jax.sharding import PartitionSpec as P

HEAD = 128
HEADS = 20
TICKS = 4


def from_behind(value, axis, steps):
    count = lax.axis_size(axis)
    pairs = [(source, (source + steps) % count) for source in range(count)]
    return lax.ppermute(value, axis, pairs)


def modulate(rows_in, shift_row, scale_row):
    average = jnp.mean(rows_in, axis=-1, keepdims=True)
    centred = rows_in - average
    variance = jnp.mean(centred * centred, axis=-1, keepdims=True)
    return centred / jnp.sqrt(variance + 1e-06) * (1.0 + scale_row) + shift_row


def head_norm(rows_in):
    shaped = rows_in.reshape(rows_in.shape[0], HEADS, HEAD)
    square = jnp.mean(shaped * shaped, axis=-1, keepdims=True)
    return (shaped / jnp.sqrt(square + 1e-06)).reshape(rows_in.shape)


def raw_scores(queries, keys_all):
    count = queries.shape[0]
    query_heads = queries.reshape(count, HEADS, HEAD)
    key_heads = keys_all.reshape(-1, HEADS, HEAD)
    return jnp.einsum(
        "rhd,khd->rhk", query_heads, key_heads, preferred_element_type=jnp.float32
    ) * HEAD ** (-0.5)


def local_terms(queries, keys_all, values_all):
    scores = raw_scores(queries, keys_all)
    highest = jnp.max(scores, axis=-1)
    weights = jnp.exp(scores - highest[:, :, None]).astype(jnp.bfloat16)
    totals = jnp.sum(weights.astype(jnp.float32), axis=-1)
    value_heads = values_all.reshape(-1, HEADS, HEAD)
    summed = jnp.einsum("rhk,khd->rhd", weights, value_heads, preferred_element_type=jnp.float32)
    return (summed, highest, totals)


def attend(queries, keys_all, values_all):
    summed, highest, totals = local_terms(queries, keys_all, values_all)
    return (summed / totals[:, :, None]).reshape(queries.shape[0], HEADS * HEAD)


def shards(hidden, kv_cache, step_index, mod_table, query_gain, key_gain):
    sections = lax.axis_size("section")
    patches = lax.axis_size("patch")
    section_now = lax.axis_index("section")
    state = hidden[0]
    rows = state.shape[0]
    width = state.shape[1]
    own_cache = kv_cache[0].reshape(sections, rows, 2, width)
    table = mod_table[:, 0]
    gain_query = query_gain[0]
    gain_key = key_gain[0]
    whole = lax.all_gather(kv_cache[0], "patch", axis=0, tiled=True).reshape(
        patches, sections, rows, 2, width
    )
    for tick_num in range(TICKS):
        micro = (section_now - tick_num) % sections
        wraps = (micro + tick_num) // sections
        stamp = jnp.sum(jnp.where(jnp.arange(sections) == micro, step_index, 0)) + wraps
        chooser = (jnp.arange(table.shape[0]) == stamp)[:, None, None]
        picked = jnp.sum(jnp.where(chooser, table, 0.0), axis=0)
        modulated = modulate(state.astype(jnp.float32), picked[0], picked[1])
        normed = head_norm(modulated)
        queries = (normed * gain_query).astype(jnp.bfloat16)
        keys_now = (normed * gain_key).astype(jnp.bfloat16)
        values_now = modulated.astype(jnp.bfloat16)
        fresh = jnp.stack([keys_now, values_now], axis=1)
        own_cache = lax.dynamic_update_slice_in_dim(own_cache, fresh[None], micro, 0)
        fresh_all = lax.all_gather(fresh, "patch", axis=0, tiled=True).reshape(
            patches, 1, rows, 2, width
        )
        whole = lax.dynamic_update_slice_in_dim(whole, fresh_all, micro, 1)
        flat = whole.reshape(-1, 2, width)
        attended = attend(queries, flat[:, 0], flat[:, 1])
        updated = (state.astype(jnp.float32) + picked[2] * attended).astype(jnp.bfloat16)
        state = from_behind(updated, "section", 1)
    return (state[None], own_cache.reshape(kv_cache.shape))


def solution(mesh):
    in_specs = (
        P("section", "patch", None),
        P("section", ("group", "patch"), None, None),
        P("group"),
        P(None, "section", None, None),
        P("section", None),
        P("section", None),
    )
    out_specs = (
        P("section", ("group", "patch"), None),
        P("section", ("group", "patch"), None, None),
    )
    return jax.shard_map(shards, mesh=mesh, in_specs=in_specs, out_specs=out_specs, check_vma=False)
```

profile of v0, /device:TPU:0, one launch (start us, length us, event | category | flops | bytes accessed | tf_op | source)
XLA Modules:
  0.0 104.0 jit_solution(3737882651409822119)
XLA Ops:
  0.6 0.9 copy.193
  1.6 0.8 convert_reduce_fusion.7
  2.4 0.7 reshape.465
  3.1 1.4 %fusion.88 = (s32[]{:T(128)}, s32[]{:T(128)}, s32[]{:T(128)}, s32[]{:T(128)}) fusion(s32[4]{0:T(128)} %param.8, s32[]{:T(128)S(6)} %select_n.89, s32[]{:T(128)S(6)} %select_n.79, s32[]{:T(128)S(6)} %select_n.74, s32[]{:T(128)S(6)} %select_n.84), kind=kLoop, calls=%fused_computation.173 | loop fusion | flops 44 | bytes 48 | tf_op jit(solution)/shard_map/reduce_sum | solution.py:71
  4.5 0.9 fusion.63
  5.5 0.7 reduce.7
  6.2 0.7 reduce.6
  9.6 0.4 fusion.27
  10.4 0.7 copy-done.2
  11.2 14.9 %all_gather.16 = bf16[8,2,2560]{2,1,0:T(2,128)(2,1)S(1)} all-gather(bf16[2,2,2560]{2,1,0:T(2,128)(2,1)S(1)} %copy.74), channel_id=1, replica_groups=mesh['group'=2,'patch'=4,'section'=4] {'patch'}, dimensions={0}, use_global_device_ids=true | all-gather | bytes 102400 | tf_op jit(solution)/shard_map/all_gather | solution.py:81
  26.1 14.7 %all-gather = bf16[1,32,2,2560]{3,2,0,1:T(2,128)(2,1)S(1)} all-gather(bf16[1,8,2,2560]{3,2,0,1:T(2,128)(2,1)S(1)} %bitcast.280), channel_id=2, replica_groups=mesh['group'=2,'patch'=4,'section'=4] {'patch'}, dimensions={1}, use_global_device_ids=true | all-gather | bytes 409600 | tf_op jit(solution)/shard_map/all_gather | solution.py:65
  40.9 1.3 %slice_reduce_fusion.7 = (bf16[32,2560]{1,0:T(8,128)(2,1)S(1)}, bf16[32,2560]{1,0:T(8,128)(2,1)S(1)}) fusion(bf16[32,2,2560]{2,1,0:T(2,128)(2,1)S(1)} %bitcast.272), kind=kLoop, calls=%fused_computation.47 | loop fusion | bytes 655360 | tf_op jit(solution)/shard_map/slice | solution.py:86
  42.3 0.3 convert_reduce_fusion.6
  43.3 2.7 %collective-permute-done = bf16[2,2560]{1,0:T(2,128)(2,1)S(1)} collective-permute-done((bf16[2,2560]{1,0:T(2,128)(2,1)S(1)}, bf16[2,2560]{1,0:T(2,128)(2,1)S(1)}, u32[]{:S(2)}, u32[]{:S(2)}) %collective-permute-start) | collective-permute-done | bytes 10272 | tf_op jit(solution)/shard_map/ppermute | solution.py:14
  46.1 0.2 fusion.58
  46.8 13.2 %all_gather.17 = bf16[8,2,2560]{2,1,0:T(2,128)(2,1)S(1)} all-gather(bf16[2,2,2560]{2,1,0:T(2,128)(2,1)S(1)} %copy.80), channel_id=1, replica_groups=mesh['group'=2,'patch'=4,'section'=4] {'patch'}, dimensions={0}, use_global_device_ids=true | all-gather | bytes 102400 | tf_op jit(solution)/shard_map/all_gather | solution.py:81
  60.1 1.3 %slice_reduce_fusion.5 = (bf16[32,2560]{1,0:T(8,128)(2,1)S(1)}, bf16[32,2560]{1,0:T(8,128)(2,1)S(1)}) fusion(bf16[32,2,2560]{2,1,0:T(2,128)(2,1)S(1)} %bitcast.273), kind=kLoop, calls=%fused_computation.45 | loop fusion | bytes 655360 | tf_op jit(solution)/shard_map/slice | solution.py:86
  61.4 0.3 convert_reduce_fusion.5
  61.8 0.2 fusion.16
  62.1 3.1 %collective-permute-done.1 = bf16[2,2560]{1,0:T(2,128)(2,1)S(1)} collective-permute-done((bf16[2,2560]{1,0:T(2,128)(2,1)S(1)}, bf16[2,2560]{1,0:T(2,128)(2,1)S(1)}, u32[]{:S(2)}, u32[]{:S(2)}) %collective-permute-start.1) | collective-permute-done | bytes 10272 | tf_op jit(solution)/shard_map/ppermute | solution.py:14
  65.2 0.2 fusion.57
  65.9 13.2 %all_gather.18 = bf16[8,2,2560]{2,1,0:T(2,128)(2,1)S(1)} all-gather(bf16[2,2,2560]{2,1,0:T(2,128)(2,1)S(1)} %copy.86), channel_id=1, replica_groups=mesh['group'=2,'patch'=4,'section'=4] {'patch'}, dimensions={0}, use_global_device_ids=true | all-gather | bytes 102400 | tf_op jit(solution)/shard_map/all_gather | solution.py:81
  79.2 1.3 %slice_reduce_fusion.3 = (bf16[32,2560]{1,0:T(8,128)(2,1)S(1)}, bf16[32,2560]{1,0:T(8,128)(2,1)S(1)}) fusion(bf16[32,2,2560]{2,1,0:T(2,128)(2,1)S(1)} %bitcast.274), kind=kLoop, calls=%fused_computation.43 | loop fusion | bytes 655360 | tf_op jit(solution)/shard_map/slice | solution.py:86
  80.6 0.3 convert_reduce_fusion.4
  80.9 0.2 fusion.10
  81.2 3.1 %collective-permute-done.2 = bf16[2,2560]{1,0:T(2,128)(2,1)S(1)} collective-permute-done((bf16[2,2560]{1,0:T(2,128)(2,1)S(1)}, bf16[2,2560]{1,0:T(2,128)(2,1)S(1)}, u32[]{:S(2)}, u32[]{:S(2)}) %collective-permute-start.2) | collective-permute-done | bytes 10272 | tf_op jit(solution)/shard_map/ppermute | solution.py:14
  84.4 0.2 fusion.56
  85.0 13.2 %all_gather.19 = bf16[8,2,2560]{2,1,0:T(2,128)(2,1)S(1)} all-gather(bf16[2,2,2560]{2,1,0:T(2,128)(2,1)S(1)} %copy.92), channel_id=1, replica_groups=mesh['group'=2,'patch'=4,'section'=4] {'patch'}, dimensions={0}, use_global_device_ids=true | all-gather | bytes 102400 | tf_op jit(solution)/shard_map/all_gather | solution.py:81
  98.3 1.3 %slice_reduce_fusion.1 = (bf16[32,2560]{1,0:T(8,128)(2,1)S(1)}, bf16[32,2560]{1,0:T(8,128)(2,1)S(1)}) fusion(bf16[32,2,2560]{2,1,0:T(2,128)(2,1)S(1)} %bitcast.275), kind=kLoop, calls=%fused_computation.41 | loop fusion | bytes 655360 | tf_op jit(solution)/shard_map/slice | solution.py:86
  99.7 0.4 convert_reduce_fusion.3
  100.3 3.0 %collective-permute-done.3 = bf16[2,2560]{1,0:T(2,128)(2,1)S(1)} collective-permute-done((bf16[2,2560]{1,0:T(2,128)(2,1)S(1)}, bf16[2,2560]{1,0:T(2,128)(2,1)S(1)}, u32[]{:S(2)}, u32[]{:S(2)}) %collective-permute-start.3) | collective-permute-done | bytes 10272 | tf_op jit(solution)/shard_map/ppermute | solution.py:14
  103.4 0.6 copy.194
  (72 shorter events, 3.6 us)
Async XLA Ops:
  0.6 8.9 %copy-start = (f32[16,1,3,2560]{3,1,2,0:T(1,128)S(1)}, f32[16,1,3,2560]{3,1,2,0:T(1,128)}, u32[]{:S(2)}) copy-start(f32[16,1,3,2560]{3,1,2,0:T(1,128)} %param.9) | copy-start | bytes 1474564
  10.3 0.7 copy-start.2
  42.8 3.1 %collective-permute-start = (bf16[2,2560]{1,0:T(2,128)(2,1)S(1)}, bf16[2,2560]{1,0:T(2,128)(2,1)S(1)}, u32[]{:S(2)}, u32[]{:S(2)}) collective-permute-start(bf16[2,2560]{1,0:T(2,128)(2,1)S(1)} %fusion.22), channel_id=1, source_target_pairs={{0,1},{1,2},{2,3},{3,0},{4,5},{5,6},{6,7},{7,4},{8,9},{9,10},{10,1... | collective-permute-start | bytes 30728 | tf_op jit(solution)/shard_map/ppermute | solution.py:14
  62.0 3.1 %collective-permute-start.1 = (bf16[2,2560]{1,0:T(2,128)(2,1)S(1)}, bf16[2,2560]{1,0:T(2,128)(2,1)S(1)}, u32[]{:S(2)}, u32[]{:S(2)}) collective-permute-start(bf16[2,2560]{1,0:T(2,128)(2,1)S(1)} %fusion.16), channel_id=1, source_target_pairs={{0,1},{1,2},{2,3},{3,0},{4,5},{5,6},{6,7},{7,4},{8,9},{9,10},{10,1... | collective-permute-start | bytes 30728 | tf_op jit(solution)/shard_map/ppermute | solution.py:14
  81.1 3.1 %collective-permute-start.2 = (bf16[2,2560]{1,0:T(2,128)(2,1)S(1)}, bf16[2,2560]{1,0:T(2,128)(2,1)S(1)}, u32[]{:S(2)}, u32[]{:S(2)}) collective-permute-start(bf16[2,2560]{1,0:T(2,128)(2,1)S(1)} %fusion.10), channel_id=1, source_target_pairs={{0,1},{1,2},{2,3},{3,0},{4,5},{5,6},{6,7},{7,4},{8,9},{9,10},{10,1... | collective-permute-start | bytes 30728 | tf_op jit(solution)/shard_map/ppermute | solution.py:14
  100.2 3.1 %collective-permute-start.3 = (bf16[2,2560]{1,0:T(2,128)(2,1)S(1)}, bf16[2,2560]{1,0:T(2,128)(2,1)S(1)}, u32[]{:S(2)}, u32[]{:S(2)}) collective-permute-start(bf16[2,2560]{1,0:T(2,128)(2,1)S(1)} %fusion.4), channel_id=1, source_target_pairs={{0,1},{1,2},{2,3},{3,0},{4,5},{5,6},{6,7},{7,4},{8,9},{9,10},{10,1... | collective-permute-start | bytes 30728 | tf_op jit(solution)/shard_map/ppermute | solution.py:14
  100.3 3.7 %copy-start.1 = (bf16[4,2,2,2560]{3,2,1,0:T(2,128)(2,1)}, bf16[4,2,2,2560]{3,2,1,0:T(2,128)(2,1)S(1)}, u32[]{:S(2)}) copy-start(bf16[4,2,2,2560]{3,2,1,0:T(2,128)(2,1)S(1)} %copy_dynamic-update-slice_fusion) | copy-start | bytes 245764
where the time goes:
time: 105 us; the launch traced here: 104 us
  blocking collectives  69.2 us (66%)
  waiting for transfers between devices  11.8 us (11%)
  local copies, waits for them, and re-layouts  9.18 us (9%)
  other arithmetic  7.79 us (7%)
  between operations  3.63 us (3%)
  matrix products  2.09 us (2%)
    all_gather x4, blocking collectives, shards(): lax.all_gather(fresh, 'patch', axis=0, tiled=True)  54.6 us
    all_gather x1, blocking collectives, shards(): lax.all_gather(kv_cache[0], 'patch', axis=0, tiled=True)  14.7 us
    ppermute x4, waiting for transfers between devices, from_behind(): return lax.ppermute(value, axis, pairs)  11.8 us
    slice x4, local copies, waits for them, and re-layouts, shards(): attended = attend(queries, flat[:, 0], flat[:, 1])  5.39 us
    unnamed x11, local copies, waits for them, and re-layouts  2.46 us
  transfers between devices with their start and end apart: 4, of which 4 were waited for; matrix products, arithmetic and copies ran while one was open for 0% of the time, Pallas kernels for 0%

commit v1 on v0

--- a/solution.py
+++ b/solution.py
@@ -1,11 +1,16 @@
 import jax
 import jax.numpy as jnp
 from jax import lax
+from jax.experimental import pallas as pl
+from jax.experimental.pallas import tpu as pltpu
 from jax.sharding import PartitionSpec as P
 
 HEAD = 128
 HEADS = 20
 TICKS = 4
+ROWS = 8
+STALE = 32
+SLOTS = STALE + TICKS * ROWS
 
 
 def from_behind(value, axis, steps):
@@ -27,31 +32,22 @@
     return (shaped / jnp.sqrt(square + 1e-06)).reshape(rows_in.shape)
 
 
-def raw_scores(queries, keys_all):
+def attend(queries, keys_all, values_all):
     count = queries.shape[0]
     query_heads = queries.reshape(count, HEADS, HEAD)
     key_heads = keys_all.reshape(-1, HEADS, HEAD)
-    return jnp.einsum(
+    value_heads = values_all.reshape(-1, HEADS, HEAD)
+    scores = jnp.einsum(
         "rhd,khd->rhk", query_heads, key_heads, preferred_element_type=jnp.float32
     ) * HEAD ** (-0.5)
-
-
-def local_terms(queries, keys_all, values_all):
-    scores = raw_scores(queries, keys_all)
     highest = jnp.max(scores, axis=-1)
     weights = jnp.exp(scores - highest[:, :, None]).astype(jnp.bfloat16)
     totals = jnp.sum(weights.astype(jnp.float32), axis=-1)
-    value_heads = values_all.reshape(-1, HEADS, HEAD)
     summed = jnp.einsum("rhk,khd->rhd", weights, value_heads, preferred_element_type=jnp.float32)
-    return (summed, highest, totals)
-
-
-def attend(queries, keys_all, values_all):
-    summed, highest, totals = local_terms(queries, keys_all, values_all)
-    return (summed / totals[:, :, None]).reshape(queries.shape[0], HEADS * HEAD)
-
-
-def shards(hidden, kv_cache, step_index, mod_table, query_gain, key_gain):
+    return (summed / totals[:, :, None]).reshape(count, HEADS * HEAD)
+
+
+def general_shards(hidden, kv_cache, step_index, mod_table, query_gain, key_gain):
     sections = lax.axis_size("section")
     patches = lax.axis_size("patch")
     section_now = lax.axis_index("section")
@@ -60,8 +56,6 @@
     width = state.shape[1]
     own_cache = kv_cache[0].reshape(sections, rows, 2, width)
     table = mod_table[:, 0]
-    gain_query = query_gain[0]
-    gain_key = key_gain[0]
     whole = lax.all_gather(kv_cache[0], "patch", axis=0, tiled=True).reshape(
         patches, sections, rows, 2, width
     )
@@ -73,10 +67,9 @@
         picked = jnp.sum(jnp.where(chooser, table, 0.0), axis=0)
         modulated = modulate(state.astype(jnp.float32), picked[0], picked[1])
         normed = head_norm(modulated)
-        queries = (normed * gain_query).astype(jnp.bfloat16)
-        keys_now = (normed * gain_key).astype(jnp.bfloat16)
-        values_now = modulated.astype(jnp.bfloat16)
-        fresh = jnp.stack([keys_now, values_now], axis=1)
+        queries = (normed * query_gain[0]).astype(jnp.bfloat16)
+        keys_now = (normed * key_gain[0]).astype(jnp.bfloat16)
+        fresh = jnp.stack([keys_now, modulated.astype(jnp.bfloat16)], axis=1)
         own_cache = lax.dynamic_update_slice_in_dim(own_cache, fresh[None], micro, 0)
         fresh_all = lax.all_gather(fresh, "patch", axis=0, tiled=True).reshape(
             patches, 1, rows, 2, width
@@ -89,6 +82,246 @@
     return (state[None], own_cache.reshape(kv_cache.shape))
 
 
+def swap(value, axis, bit):
+    count = lax.axis_size(axis)
+    return lax.ppermute(value, axis, [(source, source ^ bit) for source in range(count)])
+
+
+def project(rows_in, mods, layer, tick):
+    shift_row = mods[layer, 3 * tick]
+    scale_row = mods[layer, 3 * tick + 1]
+    average = jnp.mean(rows_in, axis=-1, keepdims=True)
+    centred = rows_in - average
+    variance = jnp.mean(centred * centred, axis=-1, keepdims=True)
+    modulated = centred * lax.rsqrt(variance + 1e-06) * (1.0 + scale_row) + shift_row
+    normed = []
+    for head in range(HEADS):
+        part = modulated[:, head * HEAD : (head + 1) * HEAD]
+        square = jnp.mean(part * part, axis=-1, keepdims=True)
+        normed.append(part * lax.rsqrt(square + 1e-06))
+    normed = jnp.concatenate(normed, axis=1)
+    queries = (normed * mods[layer, 3 * TICKS]).astype(jnp.bfloat16)
+    keys_now = (normed * mods[layer, 3 * TICKS + 1]).astype(jnp.bfloat16)
+    return queries, keys_now, modulated.astype(jnp.bfloat16)
+
+
+def refresh(keys, values, layer, tick, keys_now, values_now):
+    place = STALE + tick * ROWS
+    keys[layer, place : place + ROWS] = keys_now
+    values[layer, place : place + ROWS] = values_now
+
+
+def valid_keys(rows, tick):
+    lane = lax.broadcasted_iota(jnp.int32, (rows, SLOTS), 1)
+    stale = (lane < STALE) & (lane % 8 < 2 * (TICKS - 1 - tick))
+    fresh = (lane >= STALE) & (lane < STALE + (tick + 1) * ROWS)
+    return stale | fresh
+
+
+def attended_rows(queries, keys, values, layer, valid):
+    parts = []
+    for head in range(HEADS):
+        span = slice(head * HEAD, (head + 1) * HEAD)
+        scores = lax.dot_general(
+            queries[:, span],
+            keys[layer, :, span],
+            (((1,), (1,)), ((), ())),
+            preferred_element_type=jnp.float32,
+        )
+        if valid is not None:
+            scores = jnp.where(valid, scores, -3.0e38)
+        highest = jnp.max(scores, axis=-1, keepdims=True)
+        weights = jnp.exp((scores - highest) * HEAD ** (-0.5)).astype(jnp.bfloat16)
+        total = jnp.sum(weights.astype(jnp.float32), axis=-1, keepdims=True)
+        summed = jnp.dot(weights, values[layer, :, span], preferred_element_type=jnp.float32)
+        parts.append(summed / total)
+    return jnp.concatenate(parts, axis=1)
+
+
+def advance(rows_in, mods, layer, tick, attended):
+    gate_row = mods[layer, 3 * tick + 2]
+    return (rows_in + gate_row * attended).astype(jnp.bfloat16)
+
+
+def first_kernel(section, own, other, own_mods, other_mods, keys, values, mods, sent):
+    @pl.when(section[0] % 2 == 0)
+    def _():
+        mods[0] = own_mods[...]
+        mods[1] = other_mods[...]
+
+    @pl.when(section[0] % 2 != 0)
+    def _():
+        mods[1] = own_mods[...]
+        mods[0] = other_mods[...]
+
+    def fill(layer, chunks):
+        for index, chunk in enumerate(chunks):
+            keys[layer, index * 8 : index * 8 + 8] = chunk[0:8]
+            values[layer, index * 8 : index * 8 + 8] = chunk[8:16]
+        keys[layer, STALE:] = jnp.zeros((SLOTS - STALE, keys.shape[2]), keys.dtype)
+        values[layer, STALE:] = jnp.zeros((SLOTS - STALE, keys.shape[2]), keys.dtype)
+
+    @pl.when(section[0] % 2 == 0)
+    def _():
+        fill(0, own)
+        fill(1, other)
+
+    @pl.when(section[0] % 2 != 0)
+    def _():
+        fill(1, own)
+        fill(0, other)
+
+    def entering(layer):
+        parts = [keys[layer, index * 8 + 6 : index * 8 + 8].astype(jnp.float32) for index in range(4)]
+        return jnp.concatenate(parts, axis=0)
+
+    valid = valid_keys(ROWS, 0)
+    after = []
+    for layer in range(2):
+        rows_in = entering(layer)
+        queries, keys_now, values_now = project(rows_in, mods, layer, 0)
+        refresh(keys, values, layer, 0, keys_now, values_now)
+        attended = attended_rows(queries, keys, values, layer, valid)
+        after.append(advance(rows_in, mods, layer, 0, attended))
+    rows_in = after[0].astype(jnp.float32)
+    queries, keys_now, values_now = project(rows_in, mods, 1, 1)
+    refresh(keys, values, 1, 1, keys_now, values_now)
+    attended = attended_rows(queries, keys, values, 1, valid_keys(ROWS, 1))
+    sent[0:ROWS] = advance(rows_in, mods, 1, 1, attended)
+    sent[ROWS:] = after[1]
+
+
+def second_kernel(came, mods, keys_in, values_in, keys, values, sent):
+    keys[...] = keys_in[...]
+    values[...] = values_in[...]
+    third = came[0:ROWS].astype(jnp.float32)
+    fourth = came[ROWS:].astype(jnp.float32)
+    for layer, low in ((0, 1), (1, 2)):
+        queries_d, keys_now, values_now = project(fourth, mods, layer, low)
+        refresh(keys, values, layer, low, keys_now, values_now)
+        queries_c, keys_now, values_now = project(third, mods, layer, low + 1)
+        refresh(keys, values, layer, low + 1, keys_now, values_now)
+        queries = jnp.concatenate([queries_c, queries_d], axis=0)
+        valid = jnp.concatenate(
+            [valid_keys(ROWS, low + 1).astype(jnp.int32), valid_keys(ROWS, low).astype(jnp.int32)], axis=0
+        ) > 0
+        attended = attended_rows(queries, keys, values, layer, valid)
+        third = advance(third, mods, layer, low + 1, attended[:ROWS]).astype(jnp.float32)
+        fourth = advance(fourth, mods, layer, low, attended[ROWS:]).astype(jnp.float32)
+    sent[0:ROWS] = third.astype(jnp.bfloat16)
+    sent[ROWS:] = fourth.astype(jnp.bfloat16)
+
+
+def third_kernel(section, came, mods, keys_in, values_in, hidden, cache, keys, values):
+    rows_in = came[ROWS:].astype(jnp.float32)
+    queries, keys_now, values_now = project(rows_in, mods, 0, 3)
+    old = (TICKS - 1) * ROWS
+    keys[0, 0:old] = keys_in[0, STALE : STALE + old]
+    values[0, 0:old] = values_in[0, STALE : STALE + old]
+    keys[0, old:] = keys_now
+    values[0, old:] = values_now
+    attended = attended_rows(queries, keys, values, 0, None)
+    ended = advance(rows_in, mods, 0, 3, attended)
+
+    def emit(ended_rows, layer, keys_last, values_last):
+        hidden[...] = ended_rows
+        for tick in range(TICKS):
+            start = STALE + tick * ROWS
+            micro = lax.rem(section[0] + TICKS - tick, TICKS)
+            for part, source, last in ((0, keys_in, keys_last), (1, values_in, values_last)):
+                rows = last if tick == TICKS - 1 and last is not None else source[layer, start : start + ROWS]
+                for row in range(2):
+                    cache[micro * 2 + row, part : part + 1] = rows[row : row + 1]
+
+    @pl.when(section[0] % 2 == 0)
+    def _():
+        emit(came[0:2], 0, keys_now, values_now)
+
+    @pl.when(section[0] % 2 != 0)
+    def _():
+        emit(ended[0:2], 1, None, None)
+
+
+def pick_kernel(section, steps, table, query_gain, key_gain, out, sem):
+    copies = []
+    for tick in range(TICKS):
+        micro = lax.rem(section[0] + TICKS - tick, TICKS)
+        stamp = steps[micro] + (micro > section[0]).astype(jnp.int32)
+        copies.append(pltpu.make_async_copy(table.at[stamp], out.at[pl.ds(3 * tick, 3)], sem.at[tick]))
+    copies.append(pltpu.make_async_copy(query_gain, out.at[3 * TICKS], sem.at[TICKS]))
+    copies.append(pltpu.make_async_copy(key_gain, out.at[3 * TICKS + 1], sem.at[TICKS + 1]))
+    for copy in copies:
+        copy.start()
+    for copy in copies:
+        copy.wait()
+
+
+VMEM = pl.BlockSpec(memory_space=pltpu.VMEM)
+SMEM = pl.BlockSpec(memory_space=pltpu.SMEM)
+ANY = pl.BlockSpec(memory_space=pl.ANY)
+
+
+def call(kernel, name, out_shape, in_specs, scratch=()):
+    return pl.pallas_call(
+        kernel,
+        out_shape=out_shape,
+        in_specs=in_specs,
+        out_specs=jax.tree.map(lambda _: VMEM, out_shape),
+        scratch_shapes=list(scratch),
+        compiler_params=pltpu.CompilerParams(vmem_limit_bytes=8 << 20),
+        name=name,
+    )
+
+
+def fast_shards(hidden, kv_cache, step_index, mod_table, query_gain, key_gain):
+    width = hidden.shape[-1]
+    section_now = lax.axis_index("section")
+    section = section_now.reshape(1).astype(jnp.int32)
+    shape = jax.ShapeDtypeStruct
+    bf16 = jnp.bfloat16
+
+    cached = kv_cache[0].reshape(TICKS, 2, 2, width)
+    cached = jnp.concatenate([cached, cached], axis=0)
+    stale = lax.dynamic_slice_in_dim(cached, section_now + 1, TICKS - 1, 0)
+    stale = stale.reshape(6, 2, width)
+    pack = jnp.concatenate([stale[:, 0], hidden[0], stale[:, 1], hidden[0]], axis=0)
+    own = [pack] + [swap(pack, "patch", bit) for bit in (1, 2, 3)]
+    other = [swap(chunk, "section", 1) for chunk in own]
+
+    own_mods = call(
+        pick_kernel,
+        "pick",
+        shape((3 * TICKS + 2, 1, width), jnp.float32),
+        [SMEM, SMEM, ANY, ANY, ANY],
+        [pltpu.SemaphoreType.DMA((TICKS + 2,))],
+    )(section, step_index, mod_table.reshape(-1, 3, 1, width), query_gain, key_gain)
+    other_mods = swap(own_mods, "section", 1)
+
+    both = shape((2, SLOTS, width), bf16)
+
+    def first(section_ref, *refs):
+        first_kernel(section_ref, refs[0:4], refs[4:8], *refs[8:])
+
+    sends = shape((2 * ROWS, width), bf16)
+    mods_shape = shape((2, 3 * TICKS + 2, 1, width), jnp.float32)
+    keys, values, mods, sent = call(
+        first, "first", (both, both, mods_shape, sends), [SMEM] + [VMEM] * 10
+    )(section, *own, *other, own_mods, other_mods)
+    came = swap(sent, "section", 2)
+    keys, values, sent = call(second_kernel, "second", (both, both, sends), [VMEM] * 4)(
+        came, mods, keys, values
+    )
+    came = swap(sent, "section", 2)
+    ended, cache = call(
+        third_kernel,
+        "third",
+        (shape((2, width), bf16), shape((2 * TICKS, 2, width), bf16)),
+        [SMEM] + [VMEM] * 4,
+        [pltpu.VMEM((1, TICKS * ROWS, width), bf16)] * 2,
+    )(section, came, mods, keys, values)
+    return ended[None], cache[None]
+
+
 def solution(mesh):
     in_specs = (
         P("section", "patch", None),
@@ -102,4 +335,6 @@
         P("section", ("group", "patch"), None),
         P("section", ("group", "patch"), None, None),
     )
+    fits = mesh.shape["section"] == TICKS and mesh.shape["patch"] == 4
+    shards = fast_shards if fits else general_shards
     return jax.shard_map(shards, mesh=mesh, in_specs=in_specs, out_specs=out_specs, check_vma=False)

time: 105 us -> 53.6 us (0.51)
  blocking collectives: 69.2 us -> 0 us
  Pallas kernels: 0 us -> 29.1 us
  starting transfers between devices: 0.23 us -> 9.98 us
  local copies, waits for them, and re-layouts: 9.18 us -> 1.43 us
  other arithmetic: 7.79 us -> 1.1 us
  between operations: 3.63 us -> 0.7 us
  matrix products: 2.09 us -> 0 us
    all_gather x5 -> x0, blocking collectives: 69.2 us -> none  [the longest x4 54.6 us: shards(): lax.all_gather(fresh, 'patch', axis=0, tiled=True)]
    pallas_call x0 -> x4, Pallas kernels: none -> 29.1 us  [the longest x1 13.6 us: fast_shards(): call(first, 'first', (both, both, mods_shape, sends), [SMEM] + [VMEM] * 10)]
    ppermute x4 -> x10, starting transfers between devices: 0.23 us -> 9.98 us  [swap(): lax.ppermute(value, axis, [(source, source ^ bit) for source in range(cou...]
    slice x4 -> x1, local copies, waits for them, and re-layouts: 5.39 us -> 0.09 us  [fast_shards(): stale[:, 0]]
    reduce_sum x14 -> x0, other arithmetic: 5.01 us -> none  [the longest x4 1.52 us: modulate(): variance = jnp.mean(centred * centred, axis=-1, keepdims=True)]
    unnamed x2 -> x0, other arithmetic: 1.47 us -> none
    sub x4 -> x0, matrix products: 1.4 us -> none  [local_terms(): weights = jnp.exp(scores - highest[:, :, None]).astype(jnp.bfloat16)]
    unnamed x11 -> x10, local copies, waits for them, and re-layouts: 2.46 us -> 1.33 us
  transfers between devices with their start and end apart: 4 -> 10, of which waited for: 4 -> 6; matrix products, arithmetic and copies ran while one was open for 0% -> 0% of each run, Pallas kernels for 0% -> 1%
where the time goes in v1:
time: 53.6 us; the launch traced here: 53.4 us
  Pallas kernels  29.1 us (54%)
  waiting for transfers between devices  11.1 us (21%)
  starting transfers between devices  9.98 us (19%)
  local copies, waits for them, and re-layouts  1.43 us (3%)
  other arithmetic  1.1 us (2%)
  between operations  0.7 us (1%)
    pallas_call x1, Pallas kernels, fast_shards(): call(first, 'first', (both, both, mods_shape, sends), [SMEM] + [VMEM] * 10)  13.6 us
    ppermute x10, waiting for transfers between devices, swap(): lax.ppermute(value, axis, [(source, source ^ bit) for source in range(cou...  11.1 us
    ppermute x10, starting transfers between devices, swap(): lax.ppermute(value, axis, [(source, source ^ bit) for source in range(cou...  9.98 us
    pallas_call x1, Pallas kernels, fast_shards(): call(second_kernel, 'second', (both, both, sends), [VMEM] * 4)  9.51 us
    pallas_call x1, Pallas kernels, fast_shards(): call(third_kernel, 'third', (shape((2, width), bf16), shape((2 * TICKS, 2...  5.23 us
    unnamed x10, local copies, waits for them, and re-layouts  1.33 us
  transfers between devices with their start and end apart: 10, of which 6 were waited for; matrix products, arithmetic and copies ran while one was open for 0% of the time, Pallas kernels for 1%

profile of v1, /device:TPU:0, one launch (start us, length us, event | category | flops | bytes accessed | tf_op | source)
XLA Modules:
  0.0 53.4 jit_solution(14868399667299821754)
XLA Ops:
  0.6 0.0 copy-start
  0.6 1.0 %fusion = bf16[3,2,2,2560]{3,2,1,0:T(2,128)(2,1)S(1)} fusion(s32[]{:T(128)S(6)} %select_n.3, bf16[4,2,2,2560]{3,2,1,0:T(2,128)(2,1)} %bitcast.13), kind=kLoop, calls=%fused_computation.3 | loop fusion | flops 30720 | bytes 143364 | tf_op jit(solution)/shard_map/concatenate | solution.py:284
  1.7 0.1 fusion.1
  1.8 0.0 copy-start.4
  1.8 0.7 %copy-done.4 = bf16[1,2,2560]{2,1,0:T(2,128)(2,1)S(1)} copy-done((bf16[1,2,2560]{2,1,0:T(2,128)(2,1)S(1)}, bf16[1,2,2560]{2,1,0:T(2,128)(2,1)}, u32[]{:S(2)}) %copy-start.4) | copy-done | bytes 10264
  2.5 0.1 pad_maximum_fusion.refs_0_
  2.6 5.1 %collective-permute-start.2 = (bf16[16,2560]{1,0:T(8,128)(2,1)S(1)}, bf16[16,2560]{1,0:T(8,128)(2,1)S(1)}, u32[]{:S(2)}, u32[]{:S(2)}) collective-permute-start(bf16[16,2560]{1,0:T(8,128)(2,1)S(1)} %pad_maximum_fusion.refs_0_), channel_id=1, source_target_pairs={{0,12},{4,8},{8,4},{12,0},{1,13},{5,9},{9,5},{13,1},{2,14},{6,10},... | collective-permute-start | bytes 245768 | tf_op jit(solution)/shard_map/ppermute | solution.py:87
  7.7 0.0 collective-permute-start.1
  7.7 0.6 %collective-permute-start = (bf16[16,2560]{1,0:T(8,128)(2,1)S(1)}, bf16[16,2560]{1,0:T(8,128)(2,1)S(1)}, u32[]{:S(2)}, u32[]{:S(2)}) collective-permute-start(bf16[16,2560]{1,0:T(8,128)(2,1)S(1)} %pad_maximum_fusion.refs_0_), channel_id=1, source_target_pairs={{0,4},{4,0},{8,12},{12,8},{1,5},{5,1},{9,13},{13,9},{2,6},{6,2},{1... | collective-permute-start | bytes 245768 | tf_op jit(solution)/shard_map/ppermute | solution.py:87
  8.3 0.0 copy-done
  8.4 0.6 %copy-done.3 = s32[4]{0:T(128)S(1)} copy-done((s32[4]{0:T(128)S(1)}, s32[4]{0:T(128)}, u32[]{:S(2)}) %copy-start.3) | copy-done | bytes 40
  9.0 0.8 %pick.1.refs_8_ = f32[14,1,2560]{2,1,0:T(1,128)S(1)} custom-call(s32[1]{0:T(128)} %bitcast.section.section_ref, s32[4]{0:T(128)S(1)} %copy-done.3, f32[16,3,1,2560]{3,2,1,0:T(1,128)S(1)} %bitcast.11, f32[1,2560]{1,0:T(1,128)S(1)} %copy-done.1, f32[1,2560]{1,0:T(1,128)S(1)} %copy-done.2), custom_call_target="tpu_custom_call" | custom-call | tf_op jit(solution)/shard_map/pick/pallas_call | solution.py:291
  9.8 0.1 collective-permute-start.7
  9.9 0.5 collective-permute-start.3
  10.4 0.3 collective-permute-done.2.refs_3_
  10.6 0.0 collective-permute-start.6
  10.6 3.9 %collective-permute-done.1.refs_2_ = bf16[16,2560]{1,0:T(8,128)(2,1)S(1)} collective-permute-done((bf16[16,2560]{1,0:T(8,128)(2,1)S(1)}, bf16[16,2560]{1,0:T(8,128)(2,1)S(1)}, u32[]{:S(2)}, u32[]{:S(2)}) %collective-permute-start.1) | collective-permute-done | bytes 81952 | tf_op jit(solution)/shard_map/ppermute | solution.py:87
  14.5 0.0 collective-permute-start.5
  14.5 0.0 collective-permute-done.refs_1_
  14.5 0.5 collective-permute-start.4
  15.0 0.0 collective-permute-done.3.refs_4_
  15.0 0.0 collective-permute-done.7.refs_9_
  15.0 0.0 collective-permute-done.6.refs_7_
  15.0 0.8 %collective-permute-done.5.refs_6_ = bf16[16,2560]{1,0:T(8,128)(2,1)S(1)} collective-permute-done((bf16[16,2560]{1,0:T(8,128)(2,1)S(1)}, bf16[16,2560]{1,0:T(8,128)(2,1)S(1)}, u32[]{:S(2)}, u32[]{:S(2)}) %collective-permute-start.5) | collective-permute-done | bytes 81952 | tf_op jit(solution)/shard_map/ppermute | solution.py:87
  15.8 0.2 collective-permute-done.4.refs_5_
  15.9 13.6 %first.1 = (bf16[2,64,2560]{2,1,0:T(8,128)(2,1)S(1)}, bf16[2,64,2560]{2,1,0:T(8,128)(2,1)S(1)}, f32[2,14,1,2560]{3,2,1,0:T(1,128)S(1)}, bf16[16,2560]{1,0:T(8,128)(2,1)S(1)}) custom-call(s32[1]{0:T(128)} %bitcast.section.section_ref, bf16[16,2560]{1,0:T(8,128)(2,1)S(1)} %pad_maximum_fusion.refs_0_, bf16[16,2560]{1,0:T(8,128)(2,1)S(1)} %collective-permute-done.refs_1_, ...), custom_call_target="tpu_custom_call" | custom-call | tf_op jit(solution)/shard_map/first/pallas_call | solution.py:307
  29.5 1.6 %collective-permute-start.8 = (bf16[16,2560]{1,0:T(8,128)(2,1)S(1)}, bf16[16,2560]{1,0:T(8,128)(2,1)S(1)}, u32[]{:S(2)}, u32[]{:S(2)}) collective-permute-start(bf16[16,2560]{1,0:T(8,128)(2,1)S(1)} %get-tuple-element.11), channel_id=1, source_target_pairs={{0,2},{1,3},{2,0},{3,1},{4,6},{5,7},{6,4},{7,5},{8,10},{9,11},{10,... | collective-permute-start | bytes 245768 | tf_op jit(solution)/shard_map/ppermute | solution.py:87
  31.1 3.1 %collective-permute-done.8.came = bf16[16,2560]{1,0:T(8,128)(2,1)S(1)} collective-permute-done((bf16[16,2560]{1,0:T(8,128)(2,1)S(1)}, bf16[16,2560]{1,0:T(8,128)(2,1)S(1)}, u32[]{:S(2)}, u32[]{:S(2)}) %collective-permute-start.8) | collective-permute-done | bytes 81952 | tf_op jit(solution)/shard_map/ppermute | solution.py:87
  34.2 9.5 %second.1 = (bf16[2,64,2560]{2,1,0:T(8,128)(2,1)S(1)}, bf16[2,64,2560]{2,1,0:T(8,128)(2,1)S(1)}, bf16[16,2560]{1,0:T(8,128)(2,1)S(1)}) custom-call(bf16[16,2560]{1,0:T(8,128)(2,1)S(1)} %collective-permute-done.8.came, f32[2,14,1,2560]{3,2,1,0:T(1,128)S(1)} %get-tuple-element.12.mods, bf16[2,64,2560]{2,1,0:T(8,128)(2,1)S(1)} %get-tuple-element.13.keys_in, ...), custom_call_target="tpu_custom_call" | custom-call | tf_op jit(solution)/shard_map/second/pallas_call | solution.py:311
  43.7 1.6 %collective-permute-start.9 = (bf16[16,2560]{1,0:T(8,128)(2,1)S(1)}, bf16[16,2560]{1,0:T(8,128)(2,1)S(1)}, u32[]{:S(2)}, u32[]{:S(2)}) collective-permute-start(bf16[16,2560]{1,0:T(8,128)(2,1)S(1)} %get-tuple-element.15), channel_id=1, source_target_pairs={{0,2},{1,3},{2,0},{3,1},{4,6},{5,7},{6,4},{7,5},{8,10},{9,11},{10,... | collective-permute-start | bytes 245768 | tf_op jit(solution)/shard_map/ppermute | solution.py:87
  45.3 2.9 %collective-permute-done.9.came = bf16[16,2560]{1,0:T(8,128)(2,1)S(1)} collective-permute-done((bf16[16,2560]{1,0:T(8,128)(2,1)S(1)}, bf16[16,2560]{1,0:T(8,128)(2,1)S(1)}, u32[]{:S(2)}, u32[]{:S(2)}) %collective-permute-start.9) | collective-permute-done | bytes 81952 | tf_op jit(solution)/shard_map/ppermute | solution.py:87
  48.2 5.2 %third.1 = (bf16[2,2560]{1,0:T(2,128)(2,1)}, bf16[8,2,2560]{2,1,0:T(2,128)(2,1)}) custom-call(s32[1]{0:T(128)} %bitcast.section.section_ref, bf16[16,2560]{1,0:T(8,128)(2,1)S(1)} %collective-permute-done.9.came, f32[2,14,1,2560]{3,2,1,0:T(1,128)S(1)} %get-tuple-element.12.mods, bf16[2,64,2560]{2,1,0:T(8,128)(2,1)S(1)} %get-tuple-element.16.keys_in, ...), custom_call_target="tpu_custom_call" | custom-call | tf_op jit(solution)/shard_map/third/pallas_call | solution.py:315
  (6 shorter events, 0.0 us)
Async XLA Ops:
  0.6 7.7 %copy-start = (f32[16,1,3,2560]{3,1,2,0:T(1,128)S(1)}, f32[16,1,3,2560]{3,1,2,0:T(1,128)}, u32[]{:S(2)}) copy-start(f32[16,1,3,2560]{3,1,2,0:T(1,128)} %param.9) | copy-start | bytes 1474564
  1.8 0.7 %copy-start.4 = (bf16[1,2,2560]{2,1,0:T(2,128)(2,1)S(1)}, bf16[1,2,2560]{2,1,0:T(2,128)(2,1)}, u32[]{:S(2)}) copy-start(bf16[1,2,2560]{2,1,0:T(2,128)(2,1)} %param.6) | copy-start | bytes 30724
  2.5 5.8 %copy-start.1 = (f32[1,2560]{1,0:T(1,128)S(1)}, f32[1,2560]{1,0:T(1,128)}, u32[]{:S(2)}) copy-start(f32[1,2560]{1,0:T(1,128)} %query_gain.1) | copy-start | bytes 30724
  2.5 5.8 %copy-start.2 = (f32[1,2560]{1,0:T(1,128)S(1)}, f32[1,2560]{1,0:T(1,128)}, u32[]{:S(2)}) copy-start(f32[1,2560]{1,0:T(1,128)} %key_gain.1) | copy-start | bytes 30724
  2.6 8.1 %collective-permute-start.2 = (bf16[16,2560]{1,0:T(8,128)(2,1)S(1)}, bf16[16,2560]{1,0:T(8,128)(2,1)S(1)}, u32[]{:S(2)}, u32[]{:S(2)}) collective-permute-start(bf16[16,2560]{1,0:T(8,128)(2,1)S(1)} %pad_maximum_fusion.refs_0_), channel_id=1, source_target_pairs={{0,12},{4,8},{8,4},{12,0},{1,13},{5,9},{9,5},{13,1},{2,14},{6,10},... | collective-permute-start | bytes 245768 | tf_op jit(solution)/shard_map/ppermute | solution.py:87
  7.7 6.8 %collective-permute-start.1 = (bf16[16,2560]{1,0:T(8,128)(2,1)S(1)}, bf16[16,2560]{1,0:T(8,128)(2,1)S(1)}, u32[]{:S(2)}, u32[]{:S(2)}) collective-permute-start(bf16[16,2560]{1,0:T(8,128)(2,1)S(1)} %pad_maximum_fusion.refs_0_), channel_id=1, source_target_pairs={{0,8},{4,12},{8,0},{12,4},{1,9},{5,13},{9,1},{13,5},{2,10},{6,14},... | collective-permute-start | bytes 245768 | tf_op jit(solution)/shard_map/ppermute | solution.py:87
  7.7 6.8 %collective-permute-start = (bf16[16,2560]{1,0:T(8,128)(2,1)S(1)}, bf16[16,2560]{1,0:T(8,128)(2,1)S(1)}, u32[]{:S(2)}, u32[]{:S(2)}) collective-permute-start(bf16[16,2560]{1,0:T(8,128)(2,1)S(1)} %pad_maximum_fusion.refs_0_), channel_id=1, source_target_pairs={{0,4},{4,0},{8,12},{12,8},{1,5},{5,1},{9,13},{13,9},{2,6},{6,2},{1... | collective-permute-start | bytes 245768 | tf_op jit(solution)/shard_map/ppermute | solution.py:87
  8.3 0.7 %copy-start.3 = (s32[4]{0:T(128)S(1)}, s32[4]{0:T(128)}, u32[]{:S(2)}) copy-start(s32[4]{0:T(128)} %steps.1) | copy-start | bytes 52
  9.8 5.2 %collective-permute-start.7 = (f32[14,1,2560]{2,1,0:T(1,128)S(1)}, f32[14,1,2560]{2,1,0:T(1,128)S(1)}, u32[]{:S(2)}, u32[]{:S(2)}) collective-permute-start(f32[14,1,2560]{2,1,0:T(1,128)S(1)} %pick.1.refs_8_), channel_id=1, source_target_pairs={{0,1},{1,0},{2,3},{3,2},{4,5},{5,4},{6,7},{7,6},{8,9},{9,8},{10,11... | collective-permute-start | bytes 430088 | tf_op jit(solution)/shard_map/ppermute | solution.py:87
  9.9 5.2 %collective-permute-start.3 = (bf16[16,2560]{1,0:T(8,128)(2,1)S(1)}, bf16[16,2560]{1,0:T(8,128)(2,1)S(1)}, u32[]{:S(2)}, u32[]{:S(2)}) collective-permute-start(bf16[16,2560]{1,0:T(8,128)(2,1)S(1)} %pad_maximum_fusion.refs_0_), channel_id=1, source_target_pairs={{0,1},{1,0},{2,3},{3,2},{4,5},{5,4},{6,7},{7,6},{8,9},{9,8},{10,11... | collective-permute-start | bytes 245768 | tf_op jit(solution)/shard_map/ppermute | solution.py:87
  10.6 4.4 %collective-permute-start.6 = (bf16[16,2560]{1,0:T(8,128)(2,1)S(1)}, bf16[16,2560]{1,0:T(8,128)(2,1)S(1)}, u32[]{:S(2)}, u32[]{:S(2)}) collective-permute-start(bf16[16,2560]{1,0:T(8,128)(2,1)S(1)} %collective-permute-done.2.refs_3_), channel_id=1, source_target_pairs={{0,1},{1,0},{2,3},{3,2},{4,5},{5,4},{6,7},{7,6},{8,9},{9,8},{10,11... | collective-permute-start | bytes 245768 | tf_op jit(solution)/shard_map/ppermute | solution.py:87
  14.5 1.3 %collective-permute-start.5 = (bf16[16,2560]{1,0:T(8,128)(2,1)S(1)}, bf16[16,2560]{1,0:T(8,128)(2,1)S(1)}, u32[]{:S(2)}, u32[]{:S(2)}) collective-permute-start(bf16[16,2560]{1,0:T(8,128)(2,1)S(1)} %collective-permute-done.1.refs_2_), channel_id=1, source_target_pairs={{0,1},{1,0},{2,3},{3,2},{4,5},{5,4},{6,7},{7,6},{8,9},{9,8},{10,11... | collective-permute-start | bytes 245768 | tf_op jit(solution)/shard_map/ppermute | solution.py:87
  14.5 1.4 %collective-permute-start.4 = (bf16[16,2560]{1,0:T(8,128)(2,1)S(1)}, bf16[16,2560]{1,0:T(8,128)(2,1)S(1)}, u32[]{:S(2)}, u32[]{:S(2)}) collective-permute-start(bf16[16,2560]{1,0:T(8,128)(2,1)S(1)} %collective-permute-done.refs_1_), channel_id=1, source_target_pairs={{0,1},{1,0},{2,3},{3,2},{4,5},{5,4},{6,7},{7,6},{8,9},{9,8},{10,11... | collective-permute-start | bytes 245768 | tf_op jit(solution)/shard_map/ppermute | solution.py:87
  29.5 4.7 %collective-permute-start.8 = (bf16[16,2560]{1,0:T(8,128)(2,1)S(1)}, bf16[16,2560]{1,0:T(8,128)(2,1)S(1)}, u32[]{:S(2)}, u32[]{:S(2)}) collective-permute-start(bf16[16,2560]{1,0:T(8,128)(2,1)S(1)} %get-tuple-element.11), channel_id=1, source_target_pairs={{0,2},{1,3},{2,0},{3,1},{4,6},{5,7},{6,4},{7,5},{8,10},{9,11},{10,... | collective-permute-start | bytes 245768 | tf_op jit(solution)/shard_map/ppermute | solution.py:87
  43.7 4.5 %collective-permute-start.9 = (bf16[16,2560]{1,0:T(8,128)(2,1)S(1)}, bf16[16,2560]{1,0:T(8,128)(2,1)S(1)}, u32[]{:S(2)}, u32[]{:S(2)}) collective-permute-start(bf16[16,2560]{1,0:T(8,128)(2,1)S(1)} %get-tuple-element.15), channel_id=1, source_target_pairs={{0,2},{1,3},{2,0},{3,1},{4,6},{5,7},{6,4},{7,5},{8,10},{9,11},{10,... | collective-permute-start | bytes 245768 | tf_op jit(solution)/shard_map/ppermute | solution.py:87

commit v2 on v0

--- a/solution.py
+++ b/solution.py
@@ -1,11 +1,18 @@
 import jax
 import jax.numpy as jnp
 from jax import lax
+from jax.experimental import pallas as pl
+from jax.experimental.pallas import tpu as pltpu
 from jax.sharding import PartitionSpec as P
 
 HEAD = 128
 HEADS = 20
 TICKS = 4
+ROWS = 8
+STALE = 32
+SLOTS = STALE + TICKS * ROWS
+PIECE = 640
+CHUNK = 7 * PIECE
 
 
 def from_behind(value, axis, steps):
@@ -27,31 +34,22 @@
     return (shaped / jnp.sqrt(square + 1e-06)).reshape(rows_in.shape)
 
 
-def raw_scores(queries, keys_all):
+def attend(queries, keys_all, values_all):
     count = queries.shape[0]
     query_heads = queries.reshape(count, HEADS, HEAD)
     key_heads = keys_all.reshape(-1, HEADS, HEAD)
-    return jnp.einsum(
+    value_heads = values_all.reshape(-1, HEADS, HEAD)
+    scores = jnp.einsum(
         "rhd,khd->rhk", query_heads, key_heads, preferred_element_type=jnp.float32
     ) * HEAD ** (-0.5)
-
-
-def local_terms(queries, keys_all, values_all):
-    scores = raw_scores(queries, keys_all)
     highest = jnp.max(scores, axis=-1)
     weights = jnp.exp(scores - highest[:, :, None]).astype(jnp.bfloat16)
     totals = jnp.sum(weights.astype(jnp.float32), axis=-1)
-    value_heads = values_all.reshape(-1, HEADS, HEAD)
     summed = jnp.einsum("rhk,khd->rhd", weights, value_heads, preferred_element_type=jnp.float32)
-    return (summed, highest, totals)
-
-
-def attend(queries, keys_all, values_all):
-    summed, highest, totals = local_terms(queries, keys_all, values_all)
-    return (summed / totals[:, :, None]).reshape(queries.shape[0], HEADS * HEAD)
-
-
-def shards(hidden, kv_cache, step_index, mod_table, query_gain, key_gain):
+    return (summed / totals[:, :, None]).reshape(count, HEADS * HEAD)
+
+
+def general_shards(hidden, kv_cache, step_index, mod_table, query_gain, key_gain):
     sections = lax.axis_size("section")
     patches = lax.axis_size("patch")
     section_now = lax.axis_index("section")
@@ -60,8 +58,6 @@
     width = state.shape[1]
     own_cache = kv_cache[0].reshape(sections, rows, 2, width)
     table = mod_table[:, 0]
-    gain_query = query_gain[0]
-    gain_key = key_gain[0]
     whole = lax.all_gather(kv_cache[0], "patch", axis=0, tiled=True).reshape(
         patches, sections, rows, 2, width
     )
@@ -73,10 +69,9 @@
         picked = jnp.sum(jnp.where(chooser, table, 0.0), axis=0)
         modulated = modulate(state.astype(jnp.float32), picked[0], picked[1])
         normed = head_norm(modulated)
-        queries = (normed * gain_query).astype(jnp.bfloat16)
-        keys_now = (normed * gain_key).astype(jnp.bfloat16)
-        values_now = modulated.astype(jnp.bfloat16)
-        fresh = jnp.stack([keys_now, values_now], axis=1)
+        queries = (normed * query_gain[0]).astype(jnp.bfloat16)
+        keys_now = (normed * key_gain[0]).astype(jnp.bfloat16)
+        fresh = jnp.stack([keys_now, modulated.astype(jnp.bfloat16)], axis=1)
         own_cache = lax.dynamic_update_slice_in_dim(own_cache, fresh[None], micro, 0)
         fresh_all = lax.all_gather(fresh, "patch", axis=0, tiled=True).reshape(
             patches, 1, rows, 2, width
@@ -89,6 +84,349 @@
     return (state[None], own_cache.reshape(kv_cache.shape))
 
 
+def swap(value, axis, bit):
+    count = lax.axis_size(axis)
+    return lax.ppermute(value, axis, [(source, source ^ bit) for source in range(count)])
+
+
+def mod_row(mods, index):
+    return mods[pl.ds(index, ROWS, stride=0), :]
+
+
+def project(rows_in, mods, tick):
+    shift_row = mod_row(mods, 3 * tick)
+    scale_row = mod_row(mods, 3 * tick + 1)
+    average = jnp.mean(rows_in, axis=-1, keepdims=True)
+    centred = rows_in - average
+    variance = jnp.mean(centred * centred, axis=-1, keepdims=True)
+    modulated = centred * lax.rsqrt(variance + 1e-06) * (1.0 + scale_row) + shift_row
+    normed = []
+    for head in range(HEADS):
+        part = modulated[:, head * HEAD : (head + 1) * HEAD]
+        square = jnp.mean(part * part, axis=-1, keepdims=True)
+        normed.append(part * lax.rsqrt(square + 1e-06))
+    return modulated, jnp.concatenate(normed, axis=1)
+
+
+GROUPS = ((0, 8), (8, 16), (16, 20))
+
+
+def clear_placed(*placed):
+    for place in placed:
+        place[...] = jnp.zeros_like(place)
+
+
+def weigh(scores, tick):
+    key = lax.broadcasted_iota(jnp.int32, scores.shape, 0)
+    stale = (key < STALE) & (key % 8 < 2 * (TICKS - 1 - tick))
+    fresh = (key >= STALE) & (key < STALE + (tick + 1) * ROWS)
+    scores = jnp.where(stale | fresh, scores, -3.0e38)
+    highest = jnp.max(scores, axis=0, keepdims=True)
+    weights = jnp.exp((scores - highest) * HEAD ** (-0.5))
+    return weights.T.astype(jnp.bfloat16)
+
+
+def steps(group, keys, values):
+    made = []
+    for rows_in, mods, layer, tick, placed in group:
+        modulated, normed = project(rows_in, mods, tick)
+        slot = slice(STALE + tick * ROWS, STALE + (tick + 1) * ROWS)
+        keys[layer, slot] = (normed * mod_row(mods, 3 * TICKS + 1)).astype(jnp.bfloat16)
+        values[layer, slot] = modulated.astype(jnp.bfloat16)
+        if placed is not None:
+            made.append((normed * mod_row(mods, 3 * TICKS)).astype(jnp.bfloat16))
+    group = [entry for entry in group if entry[4] is not None]
+    for queries, (_, _, _, _, placed) in zip(made, group):
+        for place, (begin, end) in zip(placed, GROUPS):
+            for head in range(begin, end):
+                low = head - begin
+                place[low * ROWS : (low + 1) * ROWS, low * HEAD : (low + 1) * HEAD] = queries[
+                    :, head * HEAD : (head + 1) * HEAD
+                ]
+    against = (((1,), (1,)), ((), ()))
+    scores = [
+        [
+            lax.dot_general(
+                keys[layer, :, begin * HEAD : end * HEAD],
+                place[...],
+                against,
+                preferred_element_type=jnp.float32,
+            )
+            for place, (begin, end) in zip(placed, GROUPS)
+        ]
+        for _, _, layer, _, placed in group
+    ]
+    weights = [
+        [weigh(part, entry[3]) for part in parts] for parts, entry in zip(scores, group)
+    ]
+    ones = jnp.ones((SLOTS, HEAD), jnp.bfloat16)
+    results = []
+    for chosen, (rows_in, mods, layer, tick, _) in zip(weights, group):
+        parts = []
+        for part, (begin, end) in zip(chosen, GROUPS):
+            totals = jnp.dot(part, ones, preferred_element_type=jnp.float32)
+            for head in range(begin, end, 2):
+                low = (head - begin) * ROWS
+                summed = jnp.dot(
+                    part[low : low + 2 * ROWS],
+                    values[layer, :, head * HEAD : (head + 2) * HEAD],
+                    preferred_element_type=jnp.float32,
+                )
+                parts.append(summed[0:ROWS, 0:HEAD] / totals[low : low + ROWS])
+                parts.append(summed[ROWS:, HEAD:] / totals[low + ROWS : low + 2 * ROWS])
+        attended = jnp.concatenate(parts, axis=1)
+        results.append((rows_in + mod_row(mods, 3 * tick + 2) * attended).astype(jnp.bfloat16))
+    return results
+
+
+def fill(layers, keys, values, states):
+    width = keys.shape[2]
+    pieces = width // PIECE
+
+    @pl.loop(0, pieces)
+    def _(index):
+        span = pl.ds(pl.multiple_of(index * PIECE, PIECE), PIECE)
+        beside = pl.ds(pl.multiple_of(width + jnp.minimum(index, pieces - 2) * PIECE, PIECE), PIECE)
+        for layer, chunks in layers:
+            entering = []
+            for number, chunk in enumerate(chunks):
+                keys[layer, number * 8 : number * 8 + 8, span] = chunk[:, span]
+                values[layer, number * 8 : number * 8 + 8, span] = chunk[:, beside]
+                entering.append(chunk[6:8, span].astype(jnp.float32))
+            states[layer, :, span] = jnp.concatenate(entering, axis=0).astype(jnp.bfloat16)
+            values[layer, STALE:, span] = jnp.zeros((SLOTS - STALE, PIECE), values.dtype)
+
+    last = width - PIECE
+    for layer, chunks in layers:
+        for number, chunk in enumerate(chunks):
+            for pair in range(3):
+                low = number * 8 + 2 * pair
+                beside = width + pair * PIECE
+                values[layer, low : low + 2, last:] = chunk[6:8, beside : beside + PIECE]
+
+
+def load_kernel(
+    section, steps, cache, hidden, table, query_gain, key_gain, out, out_mods, stale, entering, rows, sem
+):
+    copies = [pltpu.make_async_copy(hidden.at[0], entering, sem.at[0])]
+    for later in range(1, TICKS):
+        micro = lax.rem(section[0] + later, TICKS)
+        copies.append(
+            pltpu.make_async_copy(
+                cache.at[0, pl.ds(2 * micro, 2)], stale.at[pl.ds(2 * later - 2, 2)], sem.at[later]
+            )
+        )
+    for tick in range(TICKS):
+        micro = lax.rem(section[0] + TICKS - tick, TICKS)
+        stamp = steps[micro] + (micro > section[0]).astype(jnp.int32)
+        copies.append(
+            pltpu.make_async_copy(table.at[stamp], rows.at[pl.ds(3 * tick, 3)], sem.at[TICKS + tick])
+        )
+    copies.append(pltpu.make_async_copy(query_gain, rows.at[3 * TICKS], sem.at[2 * TICKS]))
+    copies.append(pltpu.make_async_copy(key_gain, rows.at[3 * TICKS + 1], sem.at[2 * TICKS + 1]))
+    for copy in copies:
+        copy.start()
+    for copy in copies:
+        copy.wait()
+    width = entering.shape[1]
+    for place in (out, out_mods):
+        place[0:6, 0:width] = stale[:, 0]
+        place[6:8, 0:width] = entering[...]
+        place[0:6, width:CHUNK] = stale[:, 1, 0 : 3 * PIECE]
+        for pair in range(3):
+            place[6:8, width + pair * PIECE : width + (pair + 1) * PIECE] = stale[
+                2 * pair : 2 * pair + 2, 1, 3 * PIECE :
+            ]
+    upper = jnp.concatenate([rows[index] for index in range(8)], axis=0)
+    lower = [rows[index] for index in range(8, 14)]
+    split = 3 * PIECE
+    first = jnp.concatenate([row[:, 0:split] for row in lower], axis=0)
+    last = [
+        jnp.concatenate([lower[2 * pair][:, split:], lower[2 * pair + 1][:, split:]], axis=0)
+        for pair in range(3)
+    ]
+    lower = jnp.concatenate([first, jnp.concatenate(last, axis=1)], axis=0)
+    whole = jnp.concatenate([upper, lower], axis=1)
+    high = whole.astype(out.dtype)
+    out_mods[:, CHUNK : 2 * CHUNK] = high
+    out_mods[:, 2 * CHUNK :] = (whole - high.astype(jnp.float32)).astype(out.dtype)
+
+
+def keep_mods(mods, layer, chunk):
+    both = chunk[:, CHUNK : 2 * CHUNK].astype(jnp.float32) + chunk[:, 2 * CHUNK :].astype(jnp.float32)
+    width = mods.shape[2]
+    mods[layer, 0:8] = both[:, 0:width]
+    mods[layer, 8:14, 0 : 3 * PIECE] = both[0:6, width:]
+    for pair in range(3):
+        begin = width + pair * PIECE
+        mods[layer, 8 + 2 * pair : 10 + 2 * pair, 3 * PIECE :] = both[6:8, begin : begin + PIECE]
+
+
+def near_kernel(own, other, keys, values, states, mods, placed):
+    for place in placed:
+        clear_placed(*place)
+    keep_mods(mods, 0, own[0])
+    keep_mods(mods, 1, other[0])
+    fill(((0, own), (1, other)), keys, values, states)
+    states[0], states[1] = steps(
+        [
+            (states[0].astype(jnp.float32), mods.at[0], 0, 0, placed[0]),
+            (states[1].astype(jnp.float32), mods.at[1], 1, 0, placed[1]),
+        ],
+        keys,
+        values,
+    )
+
+
+def far_kernel(
+    section,
+    far,
+    across,
+    near_keys,
+    near_values,
+    near_states,
+    near_mods,
+    hidden,
+    cache,
+    keys,
+    values,
+    mods,
+    states,
+    placed,
+    sem,
+):
+    beside = jnp.where(section[0] % 2 == 0, 1, TICKS - 1)
+    cross = TICKS - beside
+    copies = [
+        pltpu.make_async_copy(near_keys.at[1], keys.at[beside], sem.at[0]),
+        pltpu.make_async_copy(near_values.at[1], values.at[beside], sem.at[1]),
+    ]
+    for copy in copies:
+        copy.start()
+    for place in placed:
+        clear_placed(*place)
+    mods[0] = near_mods[0]
+    mods[beside] = near_mods[1]
+    keep_mods(mods, 2, far[0])
+    keep_mods(mods, cross, across[0])
+    fill(((2, far), (cross, across)), keys, values, states)
+    states[0] = near_states[0]
+    states[beside] = near_states[1]
+
+    def rows(micro):
+        return states[micro].astype(jnp.float32)
+
+    states[2], states[cross] = steps(
+        [
+            (rows(2), mods.at[2], 2, 0, placed[0]),
+            (rows(cross), mods.at[cross], cross, 0, placed[1]),
+        ],
+        keys,
+        values,
+    )
+    for copy in copies:
+        copy.wait()
+    for tick in range(1, TICKS):
+        group = [
+            (rows(micro), mods.at[micro + tick], micro + tick, tick, placed[micro])
+            for micro in range(TICKS - tick)
+        ]
+        group.append((rows(TICKS - tick), mods.at[0], 0, tick, None))
+        for micro, result in enumerate(steps(group, keys, values)):
+            states[micro] = result
+    hidden[...] = states[0, 0:2]
+    for tick in range(TICKS):
+        start = STALE + tick * ROWS
+        micro = lax.rem(section[0] + TICKS - tick, TICKS)
+        pairs = ((near_keys, near_values), (keys, values))[tick > 0]
+        for part, source in enumerate(pairs):
+            made = source[0, start : start + ROWS]
+            for row in range(2):
+                cache[micro * 2 + row, part : part + 1] = made[row : row + 1]
+
+
+VMEM = pl.BlockSpec(memory_space=pltpu.VMEM)
+SMEM = pl.BlockSpec(memory_space=pltpu.SMEM)
+HBM = pl.BlockSpec(memory_space=pltpu.HBM)
+
+
+def call(kernel, out_shape, in_specs, scratch=(), limit=12 << 20):
+    return pl.pallas_call(
+        kernel,
+        out_shape=out_shape,
+        in_specs=in_specs,
+        out_specs=jax.tree.map(lambda _: VMEM, out_shape),
+        scratch_shapes=list(scratch),
+        compiler_params=pltpu.CompilerParams(vmem_limit_bytes=limit),
+    )
+
+
+def fast_shards(*arrays):
+    return fast_body(*arrays)
+
+
+def fast_body(hidden, kv_cache, step_index, mod_table, query_gain, key_gain):
+    width = hidden.shape[-1]
+    section_now = lax.axis_index("section")
+    section = section_now.reshape(1).astype(jnp.int32)
+    shape = jax.ShapeDtypeStruct
+    bf16 = jnp.bfloat16
+
+    pack, with_mods = call(
+        load_kernel,
+        (shape((8, CHUNK), bf16), shape((8, 3 * CHUNK), bf16)),
+        [SMEM, SMEM] + [HBM] * 5,
+        [
+            pltpu.VMEM((6, 2, width), bf16),
+            pltpu.VMEM((2, width), bf16),
+            pltpu.VMEM((3 * TICKS + 2, 1, width), jnp.float32),
+            pltpu.SemaphoreType.DMA((2 * TICKS + 2,)),
+        ],
+        60 << 20,
+    )(section, step_index, kv_cache, hidden, mod_table.reshape(-1, 3, 1, width), query_gain, key_gain)
+    own = [with_mods] + [swap(pack, "patch", bit) for bit in (1, 2, 3)]
+    other = [swap(chunk, "section", 1) for chunk in own]
+    far = [swap(chunk, "section", 2) for chunk in own]
+    across = [swap(chunk, "section", 1) for chunk in far]
+
+    def near(*refs):
+        near_kernel(refs[0:4], refs[4:8], *refs[8:12], (refs[12:15], refs[15:18]))
+
+    def distant(section_ref, *refs):
+        places = (refs[18:21], refs[21:24], refs[24:27])
+        far_kernel(section_ref, refs[0:4], refs[4:8], *refs[8:18], places, refs[27])
+
+    def layers(count):
+        return shape((count, SLOTS, width), bf16)
+
+    def states(count):
+        return shape((count, ROWS, width), bf16)
+
+    placed = [
+        pltpu.VMEM(((end - begin) * ROWS, (end - begin) * HEAD), bf16) for begin, end in GROUPS
+    ]
+    keys, values, after, mods = call(
+        near,
+        (layers(2), layers(2), states(2), shape((2, 16, width), jnp.float32)),
+        [VMEM] * 8,
+        placed * 2,
+    )(*own, *other)
+    ended, cache = call(
+        distant,
+        (shape((2, width), bf16), shape((2 * TICKS, 2, width), bf16)),
+        [SMEM] + [VMEM] * 12,
+        [
+            pltpu.VMEM((TICKS, SLOTS, width), bf16),
+            pltpu.VMEM((TICKS, SLOTS, width), bf16),
+            pltpu.VMEM((TICKS, 16, width), jnp.float32),
+            pltpu.VMEM((TICKS, ROWS, width), bf16),
+        ]
+        + placed * 3
+        + [pltpu.SemaphoreType.DMA((2,))],
+    )(section, *far, *across, keys, values, after, mods)
+    return ended[None], cache[None]
+
+
 def solution(mesh):
     in_specs = (
         P("section", "patch", None),
@@ -102,4 +440,6 @@
         P("section", ("group", "patch"), None),
         P("section", ("group", "patch"), None, None),
     )
+    fits = mesh.shape["section"] == TICKS and mesh.shape["patch"] == 4
+    shards = fast_shards if fits else general_shards
     return jax.shard_map(shards, mesh=mesh, in_specs=in_specs, out_specs=out_specs, check_vma=False)

time: 105 us -> 31.7 us (0.30)
  blocking collectives: 69.2 us -> 0 us
  starting transfers between devices: 0.23 us -> 10.9 us
  Pallas kernels: 0 us -> 8.32 us
  local copies, waits for them, and re-layouts: 9.18 us -> 0.93 us
  other arithmetic: 7.79 us -> 0 us
  between operations: 3.63 us -> 0.7 us
  matrix products: 2.09 us -> 0 us
  waiting for transfers between devices: 11.8 us -> 10.6 us
    all_gather x5 -> x0, blocking collectives: 69.2 us -> none  [the longest x4 54.6 us: shards(): lax.all_gather(fresh, 'patch', axis=0, tiled=True)]
    ppermute x4 -> x15, starting transfers between devices: 0.23 us -> 10.9 us  [swap(): lax.ppermute(value, axis, [(source, source ^ bit) for source in range(cou...]
    pallas_call x0 -> x3, Pallas kernels: none -> 8.32 us  [the longest x1 4.55 us: fast_body(): call(distant, (shape((2, width), bf16), shape((2 * TICKS, 2, width), bf16...]
    slice x4 -> x0, local copies, waits for them, and re-layouts: 5.39 us -> none  [shards(): attended = attend(queries, flat[:, 0], flat[:, 1])]
    reduce_sum x14 -> x0, other arithmetic: 5.01 us -> none  [the longest x4 1.52 us: modulate(): variance = jnp.mean(centred * centred, axis=-1, keepdims=True)]
    unnamed x11 -> x2, local copies, waits for them, and re-layouts: 2.46 us -> 0.93 us
    unnamed x2 -> x0, other arithmetic: 1.47 us -> none
    sub x4 -> x0, matrix products: 1.4 us -> none  [local_terms(): weights = jnp.exp(scores - highest[:, :, None]).astype(jnp.bfloat16)]
  transfers between devices with their start and end apart: 4 -> 15, of which waited for: 4 -> 6; matrix products, arithmetic and copies ran while one was open for 0% -> 0% of each run, Pallas kernels for 0% -> 4%
where the time goes in v2:
time: 31.7 us; the launch traced here: 31.4 us
  starting transfers between devices  10.9 us (34%)
  waiting for transfers between devices  10.6 us (33%)
  Pallas kernels  8.32 us (26%)
  local copies, waits for them, and re-layouts  0.93 us (3%)
  between operations  0.7 us (2%)
    ppermute x15, starting transfers between devices, swap(): lax.ppermute(value, axis, [(source, source ^ bit) for source in range(cou...  10.9 us
    ppermute x15, waiting for transfers between devices, swap(): lax.ppermute(value, axis, [(source, source ^ bit) for source in range(cou...  10.6 us
    pallas_call x1, Pallas kernels, fast_body(): call(distant, (shape((2, width), bf16), shape((2 * TICKS, 2, width), bf16...  4.55 us
    pallas_call x1, Pallas kernels, fast_body(): call(load_kernel, (shape((8, CHUNK), bf16), shape((8, 3 * CHUNK), bf16)),...  2.67 us
    pallas_call x1, Pallas kernels, fast_body(): call(near, (layers(2), layers(2), states(2), shape((2, 16, width), jnp.fl...  1.1 us
    unnamed x2, local copies, waits for them, and re-layouts  0.93 us
  transfers between devices with their start and end apart: 15, of which 6 were waited for; matrix products, arithmetic and copies ran while one was open for 0% of the time, Pallas kernels for 4%

profile of v2, /device:TPU:0, one launch (start us, length us, event | category | flops | bytes accessed | tf_op | source)
XLA Modules:
  0.0 31.4 jit_solution(8781123622827410566)
XLA Ops:
  0.6 2.7 %shard_map.77 = (bf16[8,4480]{1,0:T(8,128)(2,1)}, bf16[8,13440]{1,0:T(8,128)(2,1)}) custom-call(s32[1]{0:T(128)} %bitcast.section.section_ref, s32[4]{0:T(128)} %steps.1, bf16[1,8,2,2560]{3,2,1,0:T(2,128)(2,1)} %cache.1, bf16[1,2,2560]{2,1,0:T(2,128)(2,1)} %hidden.1, f32[16,3,1,2560]{3,2,1,0:T(1,128)} %bitcast.4, f32[1,2560]{1,0:T(1,128)} %query_gain.1, ...), custom_call_target="tpu_custom_call" | custom-call | tf_op jit(solution)/shard_map/pallas_call | solution.py:375
  3.3 3.0 %collective-permute-start = (bf16[8,13440]{1,0:T(8,128)(2,1)}, bf16[8,13440]{1,0:T(8,128)(2,1)S(1)}, u32[]{:S(2)}, u32[]{:S(2)}) collective-permute-start(bf16[8,13440]{1,0:T(8,128)(2,1)} %get-tuple-element.10.refs_0_), channel_id=1, source_target_pairs={{0,2},{1,3},{2,0},{3,1},{4,6},{5,7},{6,4},{7,5},{8,10},{9,11},{10,... | collective-permute-start | bytes 645128 | tf_op jit(solution)/shard_map/ppermute | solution.py:89
  6.3 1.6 %collective-permute-start.1 = (bf16[8,4480]{1,0:T(8,128)(2,1)}, bf16[8,4480]{1,0:T(8,128)(2,1)S(1)}, u32[]{:S(2)}, u32[]{:S(2)}) collective-permute-start(bf16[8,4480]{1,0:T(8,128)(2,1)} %get-tuple-element.11), channel_id=1, source_target_pairs={{0,4},{4,0},{8,12},{12,8},{1,5},{5,1},{9,13},{13,9},{2,6},{6,2},{1... | collective-permute-start | bytes 215048 | tf_op jit(solution)/shard_map/ppermute | solution.py:89
  7.9 2.6 %collective-permute-start.3 = (bf16[8,4480]{1,0:T(8,128)(2,1)}, bf16[8,4480]{1,0:T(8,128)(2,1)S(1)}, u32[]{:S(2)}, u32[]{:S(2)}) collective-permute-start(bf16[8,4480]{1,0:T(8,128)(2,1)} %get-tuple-element.11), channel_id=1, source_target_pairs={{0,8},{4,12},{8,0},{12,4},{1,9},{5,13},{9,1},{13,5},{2,10},{6,14},... | collective-permute-start | bytes 215048 | tf_op jit(solution)/shard_map/ppermute | solution.py:89
  10.5 0.2 collective-permute-start.5
  10.7 0.0 collective-permute-start.11
  10.7 0.2 collective-permute-done.1.refs_1_
  10.9 0.4 %collective-permute-start.12 = (bf16[8,4480]{1,0:T(8,128)(2,1)S(1)}, bf16[8,4480]{1,0:T(8,128)(2,1)S(1)}, u32[]{:S(2)}, u32[]{:S(2)}) collective-permute-start(bf16[8,4480]{1,0:T(8,128)(2,1)S(1)} %collective-permute-done.1.refs_1_), channel_id=1, source_target_pairs={{0,1},{1,0},{2,3},{3,2},{4,5},{5,4},{6,7},{7,6},{8,9},{9,8},{10,11... | collective-permute-start | bytes 215048 | tf_op jit(solution)/shard_map/ppermute | solution.py:89
  11.2 4.3 %collective-permute-done.3.refs_2_ = bf16[8,4480]{1,0:T(8,128)(2,1)S(1)} collective-permute-done((bf16[8,4480]{1,0:T(8,128)(2,1)}, bf16[8,4480]{1,0:T(8,128)(2,1)S(1)}, u32[]{:S(2)}, u32[]{:S(2)}) %collective-permute-start.3) | collective-permute-done | bytes 71712 | tf_op jit(solution)/shard_map/ppermute | solution.py:89
  15.5 0.0 collective-permute-start.13
  15.5 1.4 %collective-permute-done.5.refs_3_ = bf16[8,4480]{1,0:T(8,128)(2,1)S(1)} collective-permute-done((bf16[8,4480]{1,0:T(8,128)(2,1)}, bf16[8,4480]{1,0:T(8,128)(2,1)S(1)}, u32[]{:S(2)}, u32[]{:S(2)}) %collective-permute-start.5) | collective-permute-done | bytes 71712 | tf_op jit(solution)/shard_map/ppermute | solution.py:89
  16.9 0.0 collective-permute-start.14
  16.9 0.0 collective-permute-done.refs_0_
  17.0 0.5 %collective-permute-start.7 = (bf16[8,13440]{1,0:T(8,128)(2,1)S(1)}, bf16[8,13440]{1,0:T(8,128)(2,1)S(1)}, u32[]{:S(2)}, u32[]{:S(2)}) collective-permute-start(bf16[8,13440]{1,0:T(8,128)(2,1)S(1)} %collective-permute-done.refs_0_), channel_id=1, source_target_pairs={{0,1},{1,0},{2,3},{3,2},{4,5},{5,4},{6,7},{7,6},{8,9},{9,8},{10,11... | collective-permute-start | bytes 645128 | tf_op jit(solution)/shard_map/ppermute | solution.py:89
  17.5 0.0 collective-permute-done.12.refs_5_
  17.5 0.5 %collective-permute-start.6 = (bf16[8,4480]{1,0:T(8,128)(2,1)S(1)}, bf16[8,4480]{1,0:T(8,128)(2,1)S(1)}, u32[]{:S(2)}, u32[]{:S(2)}) collective-permute-start(bf16[8,4480]{1,0:T(8,128)(2,1)S(1)} %collective-permute-done.5.refs_3_), channel_id=1, source_target_pairs={{0,2},{1,3},{2,0},{3,1},{4,6},{5,7},{6,4},{7,5},{8,10},{9,11},{10,... | collective-permute-start | bytes 215048 | tf_op jit(solution)/shard_map/ppermute | solution.py:89
  18.0 0.0 collective-permute-done.13.refs_6_
  18.0 1.5 %collective-permute-start.2 = (bf16[8,4480]{1,0:T(8,128)(2,1)S(1)}, bf16[8,4480]{1,0:T(8,128)(2,1)S(1)}, u32[]{:S(2)}, u32[]{:S(2)}) collective-permute-start(bf16[8,4480]{1,0:T(8,128)(2,1)S(1)} %collective-permute-done.1.refs_1_), channel_id=1, source_target_pairs={{0,2},{1,3},{2,0},{3,1},{4,6},{5,7},{6,4},{7,5},{8,10},{9,11},{10,... | collective-permute-start | bytes 215048 | tf_op jit(solution)/shard_map/ppermute | solution.py:89
  19.5 0.0 collective-permute-done.14.refs_7_
  19.5 0.5 %collective-permute-start.4 = (bf16[8,4480]{1,0:T(8,128)(2,1)S(1)}, bf16[8,4480]{1,0:T(8,128)(2,1)S(1)}, u32[]{:S(2)}, u32[]{:S(2)}) collective-permute-start(bf16[8,4480]{1,0:T(8,128)(2,1)S(1)} %collective-permute-done.3.refs_2_), channel_id=1, source_target_pairs={{0,2},{1,3},{2,0},{3,1},{4,6},{5,7},{6,4},{7,5},{8,10},{9,11},{10,... | collective-permute-start | bytes 215048 | tf_op jit(solution)/shard_map/ppermute | solution.py:89
  20.0 2.5 %collective-permute-done.6.refs_3_ = bf16[8,4480]{1,0:T(8,128)(2,1)S(1)} collective-permute-done((bf16[8,4480]{1,0:T(8,128)(2,1)S(1)}, bf16[8,4480]{1,0:T(8,128)(2,1)S(1)}, u32[]{:S(2)}, u32[]{:S(2)}) %collective-permute-start.6) | collective-permute-done | bytes 71712 | tf_op jit(solution)/shard_map/ppermute | solution.py:89
  22.6 0.0 collective-permute-start.10
  22.6 1.4 %collective-permute-done.2.refs_1_ = bf16[8,4480]{1,0:T(8,128)(2,1)S(1)} collective-permute-done((bf16[8,4480]{1,0:T(8,128)(2,1)S(1)}, bf16[8,4480]{1,0:T(8,128)(2,1)S(1)}, u32[]{:S(2)}, u32[]{:S(2)}) %collective-permute-start.2) | collective-permute-done | bytes 71712 | tf_op jit(solution)/shard_map/ppermute | solution.py:89
  24.0 0.0 collective-permute-start.8
  24.0 0.8 %collective-permute-done.4.refs_2_ = bf16[8,4480]{1,0:T(8,128)(2,1)S(1)} collective-permute-done((bf16[8,4480]{1,0:T(8,128)(2,1)S(1)}, bf16[8,4480]{1,0:T(8,128)(2,1)S(1)}, u32[]{:S(2)}, u32[]{:S(2)}) %collective-permute-start.4) | collective-permute-done | bytes 71712 | tf_op jit(solution)/shard_map/ppermute | solution.py:89
  24.7 0.0 collective-permute-start.9
  24.7 0.0 collective-permute-done.11.refs_4_
  24.7 0.9 %copy-done = bf16[8,13440]{1,0:T(8,128)(2,1)S(1)} copy-done((bf16[8,13440]{1,0:T(8,128)(2,1)S(1)}, bf16[8,13440]{1,0:T(8,128)(2,1)}, u32[]{:S(2)}) %copy-start) | copy-done | bytes 215064
  25.7 1.1 %shard_map.78 = (bf16[2,64,2560]{2,1,0:T(8,128)(2,1)S(1)}, bf16[2,64,2560]{2,1,0:T(8,128)(2,1)S(1)}, bf16[2,8,2560]{2,1,0:T(8,128)(2,1)S(1)}, f32[2,16,2560]{2,1,0:T(8,128)S(1)}) custom-call(bf16[8,13440]{1,0:T(8,128)(2,1)S(1)} %copy-done, bf16[8,4480]{1,0:T(8,128)(2,1)S(1)} %collective-permute-done.1.refs_1_, ...), custom_call_target="tpu_custom_call" | custom-call | tf_op jit(solution)/shard_map/pallas_call | solution.py:408
  26.8 0.0 collective-permute-done.8.refs_5_
  26.8 0.0 collective-permute-done.9.refs_6_
  26.8 4.6 %shard_map.79 = (bf16[2,2560]{1,0:T(2,128)(2,1)}, bf16[8,2,2560]{2,1,0:T(2,128)(2,1)}) custom-call(s32[1]{0:T(128)} %bitcast.section.section_ref, bf16[8,13440]{1,0:T(8,128)(2,1)S(1)} %collective-permute-done.refs_0_, bf16[8,4480]{1,0:T(8,128)(2,1)S(1)} %collective-permute-done.2.refs_1_, bf16[8,4480]{1,0:T(8,128)(2,1)S(1)} %collective-permute-done.4.refs_2_, ...), custom_call_target="tpu_custom_call" | custom-call | tf_op jit(solution)/shard_map/pallas_call | solution.py:414
  (3 shorter events, 0.0 us)
Async XLA Ops:
  3.3 13.6 %collective-permute-start = (bf16[8,13440]{1,0:T(8,128)(2,1)}, bf16[8,13440]{1,0:T(8,128)(2,1)S(1)}, u32[]{:S(2)}, u32[]{:S(2)}) collective-permute-start(bf16[8,13440]{1,0:T(8,128)(2,1)} %get-tuple-element.10.refs_0_), channel_id=1, source_target_pairs={{0,2},{1,3},{2,0},{3,1},{4,6},{5,7},{6,4},{7,5},{8,10},{9,11},{10,... | collective-permute-start | bytes 645128 | tf_op jit(solution)/shard_map/ppermute | solution.py:89
  6.3 4.5 %collective-permute-start.1 = (bf16[8,4480]{1,0:T(8,128)(2,1)}, bf16[8,4480]{1,0:T(8,128)(2,1)S(1)}, u32[]{:S(2)}, u32[]{:S(2)}) collective-permute-start(bf16[8,4480]{1,0:T(8,128)(2,1)} %get-tuple-element.11), channel_id=1, source_target_pairs={{0,4},{4,0},{8,12},{12,8},{1,5},{5,1},{9,13},{13,9},{2,6},{6,2},{1... | collective-permute-start | bytes 215048 | tf_op jit(solution)/shard_map/ppermute | solution.py:89
  7.9 7.6 %collective-permute-start.3 = (bf16[8,4480]{1,0:T(8,128)(2,1)}, bf16[8,4480]{1,0:T(8,128)(2,1)S(1)}, u32[]{:S(2)}, u32[]{:S(2)}) collective-permute-start(bf16[8,4480]{1,0:T(8,128)(2,1)} %get-tuple-element.11), channel_id=1, source_target_pairs={{0,8},{4,12},{8,0},{12,4},{1,9},{5,13},{9,1},{13,5},{2,10},{6,14},... | collective-permute-start | bytes 215048 | tf_op jit(solution)/shard_map/ppermute | solution.py:89
  10.5 6.4 %collective-permute-start.5 = (bf16[8,4480]{1,0:T(8,128)(2,1)}, bf16[8,4480]{1,0:T(8,128)(2,1)S(1)}, u32[]{:S(2)}, u32[]{:S(2)}) collective-permute-start(bf16[8,4480]{1,0:T(8,128)(2,1)} %get-tuple-element.11), channel_id=1, source_target_pairs={{0,12},{4,8},{8,4},{12,0},{1,13},{5,9},{9,5},{13,1},{2,14},{6,10},... | collective-permute-start | bytes 215048 | tf_op jit(solution)/shard_map/ppermute | solution.py:89
  10.7 14.0 %collective-permute-start.11 = (bf16[8,13440]{1,0:T(8,128)(2,1)}, bf16[8,13440]{1,0:T(8,128)(2,1)S(1)}, u32[]{:S(2)}, u32[]{:S(2)}) collective-permute-start(bf16[8,13440]{1,0:T(8,128)(2,1)} %get-tuple-element.10.refs_0_), channel_id=1, source_target_pairs={{0,1},{1,0},{2,3},{3,2},{4,5},{5,4},{6,7},{7,6},{8,9},{9,8},{10,11... | collective-permute-start | bytes 645128 | tf_op jit(solution)/shard_map/ppermute | solution.py:89
  10.9 6.6 %collective-permute-start.12 = (bf16[8,4480]{1,0:T(8,128)(2,1)S(1)}, bf16[8,4480]{1,0:T(8,128)(2,1)S(1)}, u32[]{:S(2)}, u32[]{:S(2)}) collective-permute-start(bf16[8,4480]{1,0:T(8,128)(2,1)S(1)} %collective-permute-done.1.refs_1_), channel_id=1, source_target_pairs={{0,1},{1,0},{2,3},{3,2},{4,5},{5,4},{6,7},{7,6},{8,9},{9,8},{10,11... | collective-permute-start | bytes 215048 | tf_op jit(solution)/shard_map/ppermute | solution.py:89
  15.5 2.5 %collective-permute-start.13 = (bf16[8,4480]{1,0:T(8,128)(2,1)S(1)}, bf16[8,4480]{1,0:T(8,128)(2,1)S(1)}, u32[]{:S(2)}, u32[]{:S(2)}) collective-permute-start(bf16[8,4480]{1,0:T(8,128)(2,1)S(1)} %collective-permute-done.3.refs_2_), channel_id=1, source_target_pairs={{0,1},{1,0},{2,3},{3,2},{4,5},{5,4},{6,7},{7,6},{8,9},{9,8},{10,11... | collective-permute-start | bytes 215048 | tf_op jit(solution)/shard_map/ppermute | solution.py:89
  16.9 2.6 %collective-permute-start.14 = (bf16[8,4480]{1,0:T(8,128)(2,1)S(1)}, bf16[8,4480]{1,0:T(8,128)(2,1)S(1)}, u32[]{:S(2)}, u32[]{:S(2)}) collective-permute-start(bf16[8,4480]{1,0:T(8,128)(2,1)S(1)} %collective-permute-done.5.refs_3_), channel_id=1, source_target_pairs={{0,1},{1,0},{2,3},{3,2},{4,5},{5,4},{6,7},{7,6},{8,9},{9,8},{10,11... | collective-permute-start | bytes 215048 | tf_op jit(solution)/shard_map/ppermute | solution.py:89
  17.0 9.9 %collective-permute-start.7 = (bf16[8,13440]{1,0:T(8,128)(2,1)S(1)}, bf16[8,13440]{1,0:T(8,128)(2,1)S(1)}, u32[]{:S(2)}, u32[]{:S(2)}) collective-permute-start(bf16[8,13440]{1,0:T(8,128)(2,1)S(1)} %collective-permute-done.refs_0_), channel_id=1, source_target_pairs={{0,1},{1,0},{2,3},{3,2},{4,5},{5,4},{6,7},{7,6},{8,9},{9,8},{10,11... | collective-permute-start | bytes 645128 | tf_op jit(solution)/shard_map/ppermute | solution.py:89
  17.5 5.1 %collective-permute-start.6 = (bf16[8,4480]{1,0:T(8,128)(2,1)S(1)}, bf16[8,4480]{1,0:T(8,128)(2,1)S(1)}, u32[]{:S(2)}, u32[]{:S(2)}) collective-permute-start(bf16[8,4480]{1,0:T(8,128)(2,1)S(1)} %collective-permute-done.5.refs_3_), channel_id=1, source_target_pairs={{0,2},{1,3},{2,0},{3,1},{4,6},{5,7},{6,4},{7,5},{8,10},{9,11},{10,... | collective-permute-start | bytes 215048 | tf_op jit(solution)/shard_map/ppermute | solution.py:89
  18.0 6.0 %collective-permute-start.2 = (bf16[8,4480]{1,0:T(8,128)(2,1)S(1)}, bf16[8,4480]{1,0:T(8,128)(2,1)S(1)}, u32[]{:S(2)}, u32[]{:S(2)}) collective-permute-start(bf16[8,4480]{1,0:T(8,128)(2,1)S(1)} %collective-permute-done.1.refs_1_), channel_id=1, source_target_pairs={{0,2},{1,3},{2,0},{3,1},{4,6},{5,7},{6,4},{7,5},{8,10},{9,11},{10,... | collective-permute-start | bytes 215048 | tf_op jit(solution)/shard_map/ppermute | solution.py:89
  19.5 5.2 %collective-permute-start.4 = (bf16[8,4480]{1,0:T(8,128)(2,1)S(1)}, bf16[8,4480]{1,0:T(8,128)(2,1)S(1)}, u32[]{:S(2)}, u32[]{:S(2)}) collective-permute-start(bf16[8,4480]{1,0:T(8,128)(2,1)S(1)} %collective-permute-done.3.refs_2_), channel_id=1, source_target_pairs={{0,2},{1,3},{2,0},{3,1},{4,6},{5,7},{6,4},{7,5},{8,10},{9,11},{10,... | collective-permute-start | bytes 215048 | tf_op jit(solution)/shard_map/ppermute | solution.py:89
  22.6 4.2 %collective-permute-start.10 = (bf16[8,4480]{1,0:T(8,128)(2,1)S(1)}, bf16[8,4480]{1,0:T(8,128)(2,1)S(1)}, u32[]{:S(2)}, u32[]{:S(2)}) collective-permute-start(bf16[8,4480]{1,0:T(8,128)(2,1)S(1)} %collective-permute-done.6.refs_3_), channel_id=1, source_target_pairs={{0,1},{1,0},{2,3},{3,2},{4,5},{5,4},{6,7},{7,6},{8,9},{9,8},{10,11... | collective-permute-start | bytes 215048 | tf_op jit(solution)/shard_map/ppermute | solution.py:89
  24.0 2.8 %collective-permute-start.8 = (bf16[8,4480]{1,0:T(8,128)(2,1)S(1)}, bf16[8,4480]{1,0:T(8,128)(2,1)S(1)}, u32[]{:S(2)}, u32[]{:S(2)}) collective-permute-start(bf16[8,4480]{1,0:T(8,128)(2,1)S(1)} %collective-permute-done.2.refs_1_), channel_id=1, source_target_pairs={{0,1},{1,0},{2,3},{3,2},{4,5},{5,4},{6,7},{7,6},{8,9},{9,8},{10,11... | collective-permute-start | bytes 215048 | tf_op jit(solution)/shard_map/ppermute | solution.py:89
  24.7 2.1 %collective-permute-start.9 = (bf16[8,4480]{1,0:T(8,128)(2,1)S(1)}, bf16[8,4480]{1,0:T(8,128)(2,1)S(1)}, u32[]{:S(2)}, u32[]{:S(2)}) collective-permute-start(bf16[8,4480]{1,0:T(8,128)(2,1)S(1)} %collective-permute-done.4.refs_2_), channel_id=1, source_target_pairs={{0,1},{1,0},{2,3},{3,2},{4,5},{5,4},{6,7},{7,6},{8,9},{9,8},{10,11... | collective-permute-start | bytes 215048 | tf_op jit(solution)/shard_map/ppermute | solution.py:89
  24.7 0.9 %copy-start = (bf16[8,13440]{1,0:T(8,128)(2,1)S(1)}, bf16[8,13440]{1,0:T(8,128)(2,1)}, u32[]{:S(2)}) copy-start(bf16[8,13440]{1,0:T(8,128)(2,1)} %get-tuple-element.10.refs_0_) | copy-start | bytes 645124

commit v3 on v2

--- a/solution.py
+++ b/solution.py
@@ -179,7 +179,7 @@
     return results
 
 
-def fill(layers, keys, values, states):
+def fill(entries, keys, values, states):
     width = keys.shape[2]
     pieces = width // PIECE
 
@@ -187,22 +187,17 @@
     def _(index):
         span = pl.ds(pl.multiple_of(index * PIECE, PIECE), PIECE)
         beside = pl.ds(pl.multiple_of(width + jnp.minimum(index, pieces - 2) * PIECE, PIECE), PIECE)
-        for layer, chunks in layers:
-            entering = []
-            for number, chunk in enumerate(chunks):
-                keys[layer, number * 8 : number * 8 + 8, span] = chunk[:, span]
-                values[layer, number * 8 : number * 8 + 8, span] = chunk[:, beside]
-                entering.append(chunk[6:8, span].astype(jnp.float32))
-            states[layer, :, span] = jnp.concatenate(entering, axis=0).astype(jnp.bfloat16)
-            values[layer, STALE:, span] = jnp.zeros((SLOTS - STALE, PIECE), values.dtype)
+        for layer, number, chunk in entries:
+            keys[layer, number * 8 : number * 8 + 8, span] = chunk[:, span]
+            values[layer, number * 8 : number * 8 + 8, span] = chunk[:, beside]
+            states[layer, number * 2 : number * 2 + 2, span] = chunk[6:8, span].astype(jnp.float32)
 
     last = width - PIECE
-    for layer, chunks in layers:
-        for number, chunk in enumerate(chunks):
-            for pair in range(3):
-                low = number * 8 + 2 * pair
-                beside = width + pair * PIECE
-                values[layer, low : low + 2, last:] = chunk[6:8, beside : beside + PIECE]
+    for layer, number, chunk in entries:
+        for pair in range(3):
+            low = number * 8 + 2 * pair
+            beside = width + pair * PIECE
+            values[layer, low : low + 2, last:] = chunk[6:8, beside : beside + PIECE]
 
 
 def load_kernel(
@@ -229,14 +224,14 @@
     for copy in copies:
         copy.wait()
     width = entering.shape[1]
-    for place in (out, out_mods):
-        place[0:6, 0:width] = stale[:, 0]
-        place[6:8, 0:width] = entering[...]
-        place[0:6, width:CHUNK] = stale[:, 1, 0 : 3 * PIECE]
-        for pair in range(3):
-            place[6:8, width + pair * PIECE : width + (pair + 1) * PIECE] = stale[
-                2 * pair : 2 * pair + 2, 1, 3 * PIECE :
-            ]
+    out[0:6, 0:width] = stale[:, 0]
+    out[6:8, 0:width] = entering[...]
+    out[0:6, width:] = stale[:, 1, 0 : 3 * PIECE]
+    for pair in range(3):
+        out[6:8, width + pair * PIECE : width + (pair + 1) * PIECE] = stale[
+            2 * pair : 2 * pair + 2, 1, 3 * PIECE :
+        ]
+    out_mods[:, 0:CHUNK] = out[...]
     upper = jnp.concatenate([rows[index] for index in range(8)], axis=0)
     lower = [rows[index] for index in range(8, 14)]
     split = 3 * PIECE
@@ -262,84 +257,89 @@
         mods[layer, 8 + 2 * pair : 10 + 2 * pair, 3 * PIECE :] = both[6:8, begin : begin + PIECE]
 
 
-def near_kernel(own, other, keys, values, states, mods, placed):
-    for place in placed:
-        clear_placed(*place)
-    keep_mods(mods, 0, own[0])
-    keep_mods(mods, 1, other[0])
-    fill(((0, own), (1, other)), keys, values, states)
-    states[0], states[1] = steps(
+def stage_kernel(loaded, chunk, mods):
+    chunk[...] = loaded[:, 0:CHUNK]
+    keep_mods(mods, 0, loaded)
+
+
+def beside_of(section):
+    return jnp.where(section[0] % 2 == 0, 1, TICKS - 1)
+
+
+def places(placed, number):
+    return [place.at[number] for place in placed]
+
+
+def early_kernel(section, own, other, own_mods, keys, values, states, mods, *placed):
+    beside = beside_of(section)
+    clear_placed(*placed)
+    values[:, STALE:] = jnp.zeros((TICKS, SLOTS - STALE, values.shape[2]), values.dtype)
+    mods[0] = own_mods[0]
+    keep_mods(mods, beside, other[0])
+    fill(
+        [(0, number, chunk) for number, chunk in enumerate(own)]
+        + [(beside, number, chunk) for number, chunk in enumerate(other)],
+        keys,
+        values,
+        states,
+    )
+
+
+def near_kernel(section, late, keys, values, states, mods, *placed):
+    beside = beside_of(section)
+    fill([(beside, 3, late)], keys, values, states)
+    results = steps(
         [
-            (states[0].astype(jnp.float32), mods.at[0], 0, 0, placed[0]),
-            (states[1].astype(jnp.float32), mods.at[1], 1, 0, placed[1]),
+            (states[0], mods.at[0], 0, 0, places(placed, 0)),
+            (states[beside], mods.at[beside], beside, 0, places(placed, 1)),
         ],
         keys,
         values,
     )
-
-
-def far_kernel(
-    section,
-    far,
-    across,
-    near_keys,
-    near_values,
-    near_states,
-    near_mods,
-    hidden,
-    cache,
-    keys,
-    values,
-    mods,
-    states,
-    placed,
-    sem,
-):
-    beside = jnp.where(section[0] % 2 == 0, 1, TICKS - 1)
-    cross = TICKS - beside
-    copies = [
-        pltpu.make_async_copy(near_keys.at[1], keys.at[beside], sem.at[0]),
-        pltpu.make_async_copy(near_values.at[1], values.at[beside], sem.at[1]),
-    ]
-    for copy in copies:
-        copy.start()
-    for place in placed:
-        clear_placed(*place)
-    mods[0] = near_mods[0]
-    mods[beside] = near_mods[1]
+    states[0] = results[0].astype(jnp.float32)
+    states[beside] = results[1].astype(jnp.float32)
+
+
+def late_kernel(section, far, across, keys, values, states, mods, *placed):
+    cross = TICKS - beside_of(section)
     keep_mods(mods, 2, far[0])
     keep_mods(mods, cross, across[0])
-    fill(((2, far), (cross, across)), keys, values, states)
-    states[0] = near_states[0]
-    states[beside] = near_states[1]
-
-    def rows(micro):
-        return states[micro].astype(jnp.float32)
-
-    states[2], states[cross] = steps(
+    fill(
+        [(2, number, chunk) for number, chunk in enumerate(far)]
+        + [(cross, number, chunk) for number, chunk in enumerate(across)],
+        keys,
+        values,
+        states,
+    )
+
+
+def far_kernel(section, late, keys, values, states, mods, placed, hidden, cache):
+    cross = TICKS - beside_of(section)
+    fill([(cross, 3, late)], keys, values, states)
+    results = steps(
         [
-            (rows(2), mods.at[2], 2, 0, placed[0]),
-            (rows(cross), mods.at[cross], cross, 0, placed[1]),
+            (states[2], mods.at[2], 2, 0, places(placed, 0)),
+            (states[cross], mods.at[cross], cross, 0, places(placed, 1)),
         ],
         keys,
         values,
     )
-    for copy in copies:
-        copy.wait()
+    states[2] = results[0].astype(jnp.float32)
+    states[cross] = results[1].astype(jnp.float32)
     for tick in range(1, TICKS):
         group = [
-            (rows(micro), mods.at[micro + tick], micro + tick, tick, placed[micro])
+            (states[micro], mods.at[micro + tick], micro + tick, tick, places(placed, micro))
             for micro in range(TICKS - tick)
         ]
-        group.append((rows(TICKS - tick), mods.at[0], 0, tick, None))
-        for micro, result in enumerate(steps(group, keys, values)):
-            states[micro] = result
-    hidden[...] = states[0, 0:2]
+        group.append((states[TICKS - tick], mods.at[0], 0, tick, None))
+        results = steps(group, keys, values)
+        for micro, result in enumerate(results):
+            states[micro] = result.astype(jnp.float32)
+    hidden[...] = results[0][0:2]
     for tick in range(TICKS):
         start = STALE + tick * ROWS
         micro = lax.rem(section[0] + TICKS - tick, TICKS)
-        pairs = ((near_keys, near_values), (keys, values))[tick > 0]
-        for part, source in enumerate(pairs):
+        for part, source in enumerate((keys, values)):
             made = source[0, start : start + ROWS]
             for row in range(2):
                 cache[micro * 2 + row, part : part + 1] = made[row : row + 1]
@@ -350,13 +350,14 @@
 HBM = pl.BlockSpec(memory_space=pltpu.HBM)
 
 
-def call(kernel, out_shape, in_specs, scratch=(), limit=12 << 20):
+def call(kernel, out_shape, in_specs, scratch=(), limit=12 << 20, aliases=None):
     return pl.pallas_call(
         kernel,
         out_shape=out_shape,
         in_specs=in_specs,
         out_specs=jax.tree.map(lambda _: VMEM, out_shape),
         scratch_shapes=list(scratch),
+        input_output_aliases=aliases or {},
         compiler_params=pltpu.CompilerParams(vmem_limit_bytes=limit),
     )
 
@@ -389,41 +390,49 @@
     far = [swap(chunk, "section", 2) for chunk in own]
     across = [swap(chunk, "section", 1) for chunk in far]
 
+    staged, staged_mods = call(
+        stage_kernel, (shape((8, CHUNK), bf16), shape((1, 16, width), jnp.float32)), [VMEM]
+    )(with_mods)
+
+    kept = (
+        shape((TICKS, SLOTS, width), bf16),
+        shape((TICKS, SLOTS, width), bf16),
+        shape((TICKS, ROWS, width), jnp.float32),
+        shape((TICKS, 16, width), jnp.float32),
+    ) + tuple(shape((3, (end - begin) * ROWS, (end - begin) * HEAD), bf16) for begin, end in GROUPS)
+    count = len(kept)
+
+    def early(section_ref, *refs):
+        early_kernel(section_ref, refs[0:4], refs[4:7], *refs[7:])
+
     def near(*refs):
-        near_kernel(refs[0:4], refs[4:8], *refs[8:12], (refs[12:15], refs[15:18]))
-
-    def distant(section_ref, *refs):
-        places = (refs[18:21], refs[21:24], refs[24:27])
-        far_kernel(section_ref, refs[0:4], refs[4:8], *refs[8:18], places, refs[27])
-
-    def layers(count):
-        return shape((count, SLOTS, width), bf16)
-
-    def states(count):
-        return shape((count, ROWS, width), bf16)
-
-    placed = [
-        pltpu.VMEM(((end - begin) * ROWS, (end - begin) * HEAD), bf16) for begin, end in GROUPS
-    ]
-    keys, values, after, mods = call(
-        near,
-        (layers(2), layers(2), states(2), shape((2, 16, width), jnp.float32)),
-        [VMEM] * 8,
-        placed * 2,
-    )(*own, *other)
-    ended, cache = call(
+        near_kernel(*refs[0:2], *refs[2 + count :])
+
+    def late(section_ref, *refs):
+        late_kernel(section_ref, refs[0:4], refs[4:7], *refs[7 + count :])
+
+    def distant(*refs):
+        held = refs[2 + count : 2 + 2 * count]
+        far_kernel(*refs[0:2], *held[0:4], held[4:], *refs[2 + 2 * count :])
+
+    def passed(kernel, inputs, buffers, extra=()):
+        first = 1 + len(inputs)
+        return call(
+            kernel,
+            kept + tuple(extra),
+            [SMEM] + [VMEM] * (len(inputs) + len(buffers)),
+            aliases={first + index: index for index in range(len(buffers))},
+        )(section, *inputs, *buffers)
+
+    buffers = passed(early, (staged, *own[1:], *other[0:3], staged_mods), ())
+    buffers = passed(near, (other[3],), buffers)
+    buffers = passed(late, (*far, *across[0:3]), buffers)
+    ended, cache = passed(
         distant,
+        (across[3],),
+        buffers,
         (shape((2, width), bf16), shape((2 * TICKS, 2, width), bf16)),
-        [SMEM] + [VMEM] * 12,
-        [
-            pltpu.VMEM((TICKS, SLOTS, width), bf16),
-            pltpu.VMEM((TICKS, SLOTS, width), bf16),
-            pltpu.VMEM((TICKS, 16, width), jnp.float32),
-            pltpu.VMEM((TICKS, ROWS, width), bf16),
-        ]
-        + placed * 3
-        + [pltpu.SemaphoreType.DMA((2,))],
-    )(section, *far, *across, keys, values, after, mods)
+    )[count:]
     return ended[None], cache[None]
 
 

time: 31.7 us -> 31.2 us (0.984)
  waiting for transfers between devices: 10.6 us -> 10.1 us
    ppermute x15, waiting for transfers between devices: 10.6 us -> 10.1 us  [swap(): lax.ppermute(value, axis, [(source, source ^ bit) for source in range(cou...]
    pallas_call x2 -> x5, Pallas kernels: 5.65 us -> 5.54 us  [the longest x4 5.51 us: passed(): call(kernel, kept + tuple(extra), [SMEM] + [VMEM] * (len(inputs) + len(bu...]
  transfers between devices with their start and end apart: 15 -> 15, of which waited for: 6 -> 6; matrix products, arithmetic and copies ran while one was open for 0% -> 0% of each run, Pallas kernels for 4% -> 5%
where the time goes in v3:
time: 31.2 us; the launch traced here: 30.9 us
  starting transfers between devices  11.2 us (36%)
  waiting for transfers between devices  10.1 us (32%)
  Pallas kernels  8.07 us (26%)
  local copies, waits for them, and re-layouts  0.93 us (3%)
  between operations  0.72 us (2%)
    ppermute x15, starting transfers between devices, swap(): lax.ppermute(value, axis, [(source, source ^ bit) for source in range(cou...  11.2 us
    ppermute x15, waiting for transfers between devices, swap(): lax.ppermute(value, axis, [(source, source ^ bit) for source in range(cou...  10.1 us
    pallas_call x4, Pallas kernels, passed(): call(kernel, kept + tuple(extra), [SMEM] + [VMEM] * (len(inputs) + len(bu...  5.51 us
    pallas_call x1, Pallas kernels, fast_body(): call(load_kernel, (shape((8, CHUNK), bf16), shape((8, 3 * CHUNK), bf16)),...  2.54 us
    unnamed x2, local copies, waits for them, and re-layouts  0.93 us
  transfers between devices with their start and end apart: 15, of which 6 were waited for; matrix products, arithmetic and copies ran while one was open for 0% of the time, Pallas kernels for 5%

profile of v3, /device:TPU:0, one launch (start us, length us, event | category | flops | bytes accessed | tf_op | source)
XLA Modules:
  0.0 30.9 jit_solution(2576347684243517177)
XLA Ops:
  0.6 2.5 %shard_map.77 = (bf16[8,4480]{1,0:T(8,128)(2,1)}, bf16[8,13440]{1,0:T(8,128)(2,1)}) custom-call(s32[1]{0:T(128)} %bitcast.section.section_ref.refs_0_, s32[4]{0:T(128)} %steps.1, bf16[1,8,2,2560]{3,2,1,0:T(2,128)(2,1)} %cache.1, bf16[1,2,2560]{2,1,0:T(2,128)(2,1)} %hidden.1, f32[16,3,1,2560]{3,2,1,0:T(1,128)} %bitcast.4, f32[1,2560]{1,0:T(1,128)} %query_gain.1, ...), custom_call_target="tpu_custom_call" | custom-call | tf_op jit(solution)/shard_map/pallas_call | solution.py:376
  3.2 3.0 %collective-permute-start.3 = (bf16[8,13440]{1,0:T(8,128)(2,1)}, bf16[8,13440]{1,0:T(8,128)(2,1)S(1)}, u32[]{:S(2)}, u32[]{:S(2)}) collective-permute-start(bf16[8,13440]{1,0:T(8,128)(2,1)} %get-tuple-element.30.loaded), channel_id=1, source_target_pairs={{0,2},{1,3},{2,0},{3,1},{4,6},{5,7},{6,4},{7,5},{8,10},{9,11},{10,... | collective-permute-start | bytes 645128 | tf_op jit(solution)/shard_map/ppermute | solution.py:89
  6.2 1.6 %collective-permute-start.4 = (bf16[8,4480]{1,0:T(8,128)(2,1)}, bf16[8,4480]{1,0:T(8,128)(2,1)S(1)}, u32[]{:S(2)}, u32[]{:S(2)}) collective-permute-start(bf16[8,4480]{1,0:T(8,128)(2,1)} %get-tuple-element.29), channel_id=1, source_target_pairs={{0,4},{4,0},{8,12},{12,8},{1,5},{5,1},{9,13},{13,9},{2,6},{6,2},{1... | collective-permute-start | bytes 215048 | tf_op jit(solution)/shard_map/ppermute | solution.py:89
  7.8 2.6 %collective-permute-start.6 = (bf16[8,4480]{1,0:T(8,128)(2,1)}, bf16[8,4480]{1,0:T(8,128)(2,1)S(1)}, u32[]{:S(2)}, u32[]{:S(2)}) collective-permute-start(bf16[8,4480]{1,0:T(8,128)(2,1)} %get-tuple-element.29), channel_id=1, source_target_pairs={{0,8},{4,12},{8,0},{12,4},{1,9},{5,13},{9,1},{13,5},{2,10},{6,14},... | collective-permute-start | bytes 215048 | tf_op jit(solution)/shard_map/ppermute | solution.py:89
  10.4 0.0 collective-permute-start.12
  10.4 0.2 collective-permute-start
  10.6 0.2 collective-permute-done.4.refs_1_
  10.7 0.1 collective-permute-start.13
  10.9 3.3 %collective-permute-done.6.refs_2_ = bf16[8,4480]{1,0:T(8,128)(2,1)S(1)} collective-permute-done((bf16[8,4480]{1,0:T(8,128)(2,1)}, bf16[8,4480]{1,0:T(8,128)(2,1)S(1)}, u32[]{:S(2)}, u32[]{:S(2)}) %collective-permute-start.6) | collective-permute-done | bytes 71712 | tf_op jit(solution)/shard_map/ppermute | solution.py:89
  14.2 0.0 collective-permute-start.14
  14.2 0.0 collective-permute-done.3.refs_0_
  14.2 0.5 %collective-permute-start.8 = (bf16[8,13440]{1,0:T(8,128)(2,1)S(1)}, bf16[8,13440]{1,0:T(8,128)(2,1)S(1)}, u32[]{:S(2)}, u32[]{:S(2)}) collective-permute-start(bf16[8,13440]{1,0:T(8,128)(2,1)S(1)} %collective-permute-done.3.refs_0_), channel_id=1, source_target_pairs={{0,1},{1,0},{2,3},{3,2},{4,5},{5,4},{6,7},{7,6},{8,9},{9,8},{10,11... | collective-permute-start | bytes 645128 | tf_op jit(solution)/shard_map/ppermute | solution.py:89
  14.7 2.3 %collective-permute-done.refs_3_ = bf16[8,4480]{1,0:T(8,128)(2,1)S(1)} collective-permute-done((bf16[8,4480]{1,0:T(8,128)(2,1)}, bf16[8,4480]{1,0:T(8,128)(2,1)S(1)}, u32[]{:S(2)}, u32[]{:S(2)}) %collective-permute-start) | collective-permute-done | bytes 71712 | tf_op jit(solution)/shard_map/ppermute | solution.py:89
  17.1 0.5 %collective-permute-start.7 = (bf16[8,4480]{1,0:T(8,128)(2,1)S(1)}, bf16[8,4480]{1,0:T(8,128)(2,1)S(1)}, u32[]{:S(2)}, u32[]{:S(2)}) collective-permute-start(bf16[8,4480]{1,0:T(8,128)(2,1)S(1)} %collective-permute-done.6.refs_2_), channel_id=1, source_target_pairs={{0,2},{1,3},{2,0},{3,1},{4,6},{5,7},{6,4},{7,5},{8,10},{9,11},{10,... | collective-permute-start | bytes 215048 | tf_op jit(solution)/shard_map/ppermute | solution.py:89
  17.6 0.0 collective-permute-done.13.refs_5_
  17.6 1.5 %collective-permute-start.5 = (bf16[8,4480]{1,0:T(8,128)(2,1)S(1)}, bf16[8,4480]{1,0:T(8,128)(2,1)S(1)}, u32[]{:S(2)}, u32[]{:S(2)}) collective-permute-start(bf16[8,4480]{1,0:T(8,128)(2,1)S(1)} %collective-permute-done.4.refs_1_), channel_id=1, source_target_pairs={{0,2},{1,3},{2,0},{3,1},{4,6},{5,7},{6,4},{7,5},{8,10},{9,11},{10,... | collective-permute-start | bytes 215048 | tf_op jit(solution)/shard_map/ppermute | solution.py:89
  19.1 0.5 %collective-permute-start.1 = (bf16[8,4480]{1,0:T(8,128)(2,1)S(1)}, bf16[8,4480]{1,0:T(8,128)(2,1)S(1)}, u32[]{:S(2)}, u32[]{:S(2)}) collective-permute-start(bf16[8,4480]{1,0:T(8,128)(2,1)S(1)} %collective-permute-done.refs_3_), channel_id=1, source_target_pairs={{0,2},{1,3},{2,0},{3,1},{4,6},{5,7},{6,4},{7,5},{8,10},{9,11},{10,... | collective-permute-start | bytes 215048 | tf_op jit(solution)/shard_map/ppermute | solution.py:89
  19.6 2.5 %collective-permute-done.7.refs_2_ = bf16[8,4480]{1,0:T(8,128)(2,1)S(1)} collective-permute-done((bf16[8,4480]{1,0:T(8,128)(2,1)S(1)}, bf16[8,4480]{1,0:T(8,128)(2,1)S(1)}, u32[]{:S(2)}, u32[]{:S(2)}) %collective-permute-start.7) | collective-permute-done | bytes 71712 | tf_op jit(solution)/shard_map/ppermute | solution.py:89
  22.2 0.0 collective-permute-start.11
  22.2 0.9 %collective-permute-done.5.refs_1_ = bf16[8,4480]{1,0:T(8,128)(2,1)S(1)} collective-permute-done((bf16[8,4480]{1,0:T(8,128)(2,1)S(1)}, bf16[8,4480]{1,0:T(8,128)(2,1)S(1)}, u32[]{:S(2)}, u32[]{:S(2)}) %collective-permute-start.5) | collective-permute-done | bytes 71712 | tf_op jit(solution)/shard_map/ppermute | solution.py:89
  23.1 0.0 collective-permute-start.10
  23.1 0.8 %collective-permute-done.1.refs_3_ = bf16[8,4480]{1,0:T(8,128)(2,1)S(1)} collective-permute-done((bf16[8,4480]{1,0:T(8,128)(2,1)S(1)}, bf16[8,4480]{1,0:T(8,128)(2,1)S(1)}, u32[]{:S(2)}, u32[]{:S(2)}) %collective-permute-start.1) | collective-permute-done | bytes 71712 | tf_op jit(solution)/shard_map/ppermute | solution.py:89
  23.9 0.0 collective-permute-start.9
  23.9 0.0 collective-permute-done.12.refs_4_
  23.9 0.5 %collective-permute-start.2 = (bf16[8,4480]{1,0:T(8,128)(2,1)S(1)}, bf16[8,4480]{1,0:T(8,128)(2,1)S(1)}, u32[]{:S(2)}, u32[]{:S(2)}) collective-permute-start(bf16[8,4480]{1,0:T(8,128)(2,1)S(1)} %collective-permute-done.1.refs_3_), channel_id=1, source_target_pairs={{0,1},{1,0},{2,3},{3,2},{4,5},{5,4},{6,7},{7,6},{8,9},{9,8},{10,11... | collective-permute-start | bytes 215048 | tf_op jit(solution)/shard_map/ppermute | solution.py:89
  24.4 0.9 %copy-done = bf16[8,13440]{1,0:T(8,128)(2,1)S(1)} copy-done((bf16[8,13440]{1,0:T(8,128)(2,1)S(1)}, bf16[8,13440]{1,0:T(8,128)(2,1)}, u32[]{:S(2)}) %copy-start) | copy-done | bytes 215064
  25.3 0.3 shard_map.79
  25.6 1.0 %shard_map.80 = (bf16[4,64,2560]{2,1,0:T(8,128)(2,1)S(1)}, bf16[4,64,2560]{2,1,0:T(8,128)(2,1)S(1)}, f32[4,8,2560]{2,1,0:T(8,128)S(1)}, f32[4,16,2560]{2,1,0:T(8...) custom-call(s32[1]{0:T(128)} %bitcast.section.section_ref.refs_0_, ...), custom_call_target="tpu_custom_call", output_to_operand_aliasing={{0}: (2, {}), {1}: (3, {}), {2}: (4, {}), {3}: (5, {}), {4}... | custom-call | tf_op jit(solution)/shard_map/pallas_call | solution.py:420
  26.6 0.0 collective-permute-done.9.refs_5_
  26.6 0.0 collective-permute-done.8.refs_4_
  26.6 0.2 shard_map.81
  26.9 4.1 %shard_map.82 = (bf16[4,64,2560]{2,1,0:T(8,128)(2,1)S(1)}, bf16[4,64,2560]{2,1,0:T(8,128)(2,1)S(1)}, f32[4,8,2560]{2,1,0:T(8,128)S(1)}, f32[4,16,2560]{2,1,0:T(8...) custom-call(s32[1]{0:T(128)} %bitcast.section.section_ref.refs_0_, ...), custom_call_target="tpu_custom_call", output_to_operand_aliasing={{0}: (2, {}), {1}: (3, {}), {2}: (4, {}), {3}: (5, {}), {4}... | custom-call | tf_op jit(solution)/shard_map/pallas_call | solution.py:420
  (6 shorter events, 0.0 us)
Async XLA Ops:
  3.2 11.0 %collective-permute-start.3 = (bf16[8,13440]{1,0:T(8,128)(2,1)}, bf16[8,13440]{1,0:T(8,128)(2,1)S(1)}, u32[]{:S(2)}, u32[]{:S(2)}) collective-permute-start(bf16[8,13440]{1,0:T(8,128)(2,1)} %get-tuple-element.30.loaded), channel_id=1, source_target_pairs={{0,2},{1,3},{2,0},{3,1},{4,6},{5,7},{6,4},{7,5},{8,10},{9,11},{10,... | collective-permute-start | bytes 645128 | tf_op jit(solution)/shard_map/ppermute | solution.py:89
  6.2 4.5 %collective-permute-start.4 = (bf16[8,4480]{1,0:T(8,128)(2,1)}, bf16[8,4480]{1,0:T(8,128)(2,1)S(1)}, u32[]{:S(2)}, u32[]{:S(2)}) collective-permute-start(bf16[8,4480]{1,0:T(8,128)(2,1)} %get-tuple-element.29), channel_id=1, source_target_pairs={{0,4},{4,0},{8,12},{12,8},{1,5},{5,1},{9,13},{13,9},{2,6},{6,2},{1... | collective-permute-start | bytes 215048 | tf_op jit(solution)/shard_map/ppermute | solution.py:89
  7.8 6.4 %collective-permute-start.6 = (bf16[8,4480]{1,0:T(8,128)(2,1)}, bf16[8,4480]{1,0:T(8,128)(2,1)S(1)}, u32[]{:S(2)}, u32[]{:S(2)}) collective-permute-start(bf16[8,4480]{1,0:T(8,128)(2,1)} %get-tuple-element.29), channel_id=1, source_target_pairs={{0,8},{4,12},{8,0},{12,4},{1,9},{5,13},{9,1},{13,5},{2,10},{6,14},... | collective-permute-start | bytes 215048 | tf_op jit(solution)/shard_map/ppermute | solution.py:89
  10.4 13.5 %collective-permute-start.12 = (bf16[8,13440]{1,0:T(8,128)(2,1)}, bf16[8,13440]{1,0:T(8,128)(2,1)S(1)}, u32[]{:S(2)}, u32[]{:S(2)}) collective-permute-start(bf16[8,13440]{1,0:T(8,128)(2,1)} %get-tuple-element.30.loaded), channel_id=1, source_target_pairs={{0,1},{1,0},{2,3},{3,2},{4,5},{5,4},{6,7},{7,6},{8,9},{9,8},{10,11... | collective-permute-start | bytes 645128 | tf_op jit(solution)/shard_map/ppermute | solution.py:89
  10.4 6.7 %collective-permute-start = (bf16[8,4480]{1,0:T(8,128)(2,1)}, bf16[8,4480]{1,0:T(8,128)(2,1)S(1)}, u32[]{:S(2)}, u32[]{:S(2)}) collective-permute-start(bf16[8,4480]{1,0:T(8,128)(2,1)} %get-tuple-element.29), channel_id=1, source_target_pairs={{0,12},{4,8},{8,4},{12,0},{1,13},{5,9},{9,5},{13,1},{2,14},{6,10},... | collective-permute-start | bytes 215048 | tf_op jit(solution)/shard_map/ppermute | solution.py:89
  10.7 6.9 %collective-permute-start.13 = (bf16[8,4480]{1,0:T(8,128)(2,1)S(1)}, bf16[8,4480]{1,0:T(8,128)(2,1)S(1)}, u32[]{:S(2)}, u32[]{:S(2)}) collective-permute-start(bf16[8,4480]{1,0:T(8,128)(2,1)S(1)} %collective-permute-done.4.refs_1_), channel_id=1, source_target_pairs={{0,1},{1,0},{2,3},{3,2},{4,5},{5,4},{6,7},{7,6},{8,9},{9,8},{10,11... | collective-permute-start | bytes 215048 | tf_op jit(solution)/shard_map/ppermute | solution.py:89
  14.2 4.9 %collective-permute-start.14 = (bf16[8,4480]{1,0:T(8,128)(2,1)S(1)}, bf16[8,4480]{1,0:T(8,128)(2,1)S(1)}, u32[]{:S(2)}, u32[]{:S(2)}) collective-permute-start(bf16[8,4480]{1,0:T(8,128)(2,1)S(1)} %collective-permute-done.6.refs_2_), channel_id=1, source_target_pairs={{0,1},{1,0},{2,3},{3,2},{4,5},{5,4},{6,7},{7,6},{8,9},{9,8},{10,11... | collective-permute-start | bytes 215048 | tf_op jit(solution)/shard_map/ppermute | solution.py:89
  14.2 12.4 %collective-permute-start.8 = (bf16[8,13440]{1,0:T(8,128)(2,1)S(1)}, bf16[8,13440]{1,0:T(8,128)(2,1)S(1)}, u32[]{:S(2)}, u32[]{:S(2)}) collective-permute-start(bf16[8,13440]{1,0:T(8,128)(2,1)S(1)} %collective-permute-done.3.refs_0_), channel_id=1, source_target_pairs={{0,1},{1,0},{2,3},{3,2},{4,5},{5,4},{6,7},{7,6},{8,9},{9,8},{10,11... | collective-permute-start | bytes 645128 | tf_op jit(solution)/shard_map/ppermute | solution.py:89
  17.1 5.1 %collective-permute-start.7 = (bf16[8,4480]{1,0:T(8,128)(2,1)S(1)}, bf16[8,4480]{1,0:T(8,128)(2,1)S(1)}, u32[]{:S(2)}, u32[]{:S(2)}) collective-permute-start(bf16[8,4480]{1,0:T(8,128)(2,1)S(1)} %collective-permute-done.6.refs_2_), channel_id=1, source_target_pairs={{0,2},{1,3},{2,0},{3,1},{4,6},{5,7},{6,4},{7,5},{8,10},{9,11},{10,... | collective-permute-start | bytes 215048 | tf_op jit(solution)/shard_map/ppermute | solution.py:89
  17.6 5.5 %collective-permute-start.5 = (bf16[8,4480]{1,0:T(8,128)(2,1)S(1)}, bf16[8,4480]{1,0:T(8,128)(2,1)S(1)}, u32[]{:S(2)}, u32[]{:S(2)}) collective-permute-start(bf16[8,4480]{1,0:T(8,128)(2,1)S(1)} %collective-permute-done.4.refs_1_), channel_id=1, source_target_pairs={{0,2},{1,3},{2,0},{3,1},{4,6},{5,7},{6,4},{7,5},{8,10},{9,11},{10,... | collective-permute-start | bytes 215048 | tf_op jit(solution)/shard_map/ppermute | solution.py:89
  19.1 4.8 %collective-permute-start.1 = (bf16[8,4480]{1,0:T(8,128)(2,1)S(1)}, bf16[8,4480]{1,0:T(8,128)(2,1)S(1)}, u32[]{:S(2)}, u32[]{:S(2)}) collective-permute-start(bf16[8,4480]{1,0:T(8,128)(2,1)S(1)} %collective-permute-done.refs_3_), channel_id=1, source_target_pairs={{0,2},{1,3},{2,0},{3,1},{4,6},{5,7},{6,4},{7,5},{8,10},{9,11},{10,... | collective-permute-start | bytes 215048 | tf_op jit(solution)/shard_map/ppermute | solution.py:89
  22.2 3.5 %collective-permute-start.11 = (bf16[8,4480]{1,0:T(8,128)(2,1)S(1)}, bf16[8,4480]{1,0:T(8,128)(2,1)S(1)}, u32[]{:S(2)}, u32[]{:S(2)}) collective-permute-start(bf16[8,4480]{1,0:T(8,128)(2,1)S(1)} %collective-permute-done.refs_3_), channel_id=1, source_target_pairs={{0,1},{1,0},{2,3},{3,2},{4,5},{5,4},{6,7},{7,6},{8,9},{9,8},{10,11... | collective-permute-start | bytes 215048 | tf_op jit(solution)/shard_map/ppermute | solution.py:89
  23.1 3.5 %collective-permute-start.10 = (bf16[8,4480]{1,0:T(8,128)(2,1)S(1)}, bf16[8,4480]{1,0:T(8,128)(2,1)S(1)}, u32[]{:S(2)}, u32[]{:S(2)}) collective-permute-start(bf16[8,4480]{1,0:T(8,128)(2,1)S(1)} %collective-permute-done.7.refs_2_), channel_id=1, source_target_pairs={{0,1},{1,0},{2,3},{3,2},{4,5},{5,4},{6,7},{7,6},{8,9},{9,8},{10,11... | collective-permute-start | bytes 215048 | tf_op jit(solution)/shard_map/ppermute | solution.py:89
  23.9 2.7 %collective-permute-start.9 = (bf16[8,4480]{1,0:T(8,128)(2,1)S(1)}, bf16[8,4480]{1,0:T(8,128)(2,1)S(1)}, u32[]{:S(2)}, u32[]{:S(2)}) collective-permute-start(bf16[8,4480]{1,0:T(8,128)(2,1)S(1)} %collective-permute-done.5.refs_1_), channel_id=1, source_target_pairs={{0,1},{1,0},{2,3},{3,2},{4,5},{5,4},{6,7},{7,6},{8,9},{9,8},{10,11... | collective-permute-start | bytes 215048 | tf_op jit(solution)/shard_map/ppermute | solution.py:89
  23.9 3.0 %collective-permute-start.2 = (bf16[8,4480]{1,0:T(8,128)(2,1)S(1)}, bf16[8,4480]{1,0:T(8,128)(2,1)S(1)}, u32[]{:S(2)}, u32[]{:S(2)}) collective-permute-start(bf16[8,4480]{1,0:T(8,128)(2,1)S(1)} %collective-permute-done.1.refs_3_), channel_id=1, source_target_pairs={{0,1},{1,0},{2,3},{3,2},{4,5},{5,4},{6,7},{7,6},{8,9},{9,8},{10,11... | collective-permute-start | bytes 215048 | tf_op jit(solution)/shard_map/ppermute | solution.py:89
  24.4 0.9 %copy-start = (bf16[8,13440]{1,0:T(8,128)(2,1)S(1)}, bf16[8,13440]{1,0:T(8,128)(2,1)}, u32[]{:S(2)}) copy-start(bf16[8,13440]{1,0:T(8,128)(2,1)} %get-tuple-element.30.loaded) | copy-start | bytes 645124
